TPU v7x, 512 devices: a whole 4x4x16 slice. The times are simulated.
512 devices in a mesh: loop: 64 (over z, x_hi, core), narrow: 8 (over x_lo, y).
Axes of the slice: x: 4 (x_hi: 2, x_lo: 2; x = x_hi * 2 + x_lo), y: 4, z: 16, core: 2. Of those that a mesh axis runs over, the one named last changes fastest.
Arguments:
- tokens: bfloat16 [1024, 8192], P('loop', 'narrow'), may hold values from -6 to 6
- gate_weight: bfloat16 [8192, 28672], P('narrow', 'loop'), may hold values from -0.0625 to 0.0625
- up_weight: bfloat16 [8192, 28672], P('narrow', 'loop'), may hold values from -0.0625 to 0.0625
- down_weight: bfloat16 [28672, 8192], P('loop', 'narrow'), may hold values from -0.03125 to 0.03125
Outputs:
- mixed: bfloat16 [1024, 8192], P('loop', 'narrow')
All inputs are finite; a program needn't handle non-finite values.
Results may differ from a plain program's by a relative error of at most 0.0049.
Values may be sent and summed in bfloat16 or wider, within the bound.
No kernel may reach another device: no remote copies, remote signals or barrier semaphores. Data moves between devices by JAX's collectives and lax.ppermute only.
A program may use at most 64 MiB of HBM per device.

v0:
```python
import jax
import jax.numpy as jnp
from jax import lax
from jax.sharding import PartitionSpec as P


def shards(tokens, gate_weight, up_weight, down_weight):
    width = gate_weight.shape[1]
    block_rows = lax.all_gather(tokens, "loop", axis=0, tiled=True)
    partial_sums = jnp.concatenate(
        (
            jnp.dot(block_rows, gate_weight, preferred_element_type=jnp.float32),
            jnp.dot(block_rows, up_weight, preferred_element_type=jnp.float32),
        ),
        axis=1,
    )
    totals = lax.psum(partial_sums, "narrow")
    hidden = (jax.nn.silu(totals[:, :width]) * totals[:, width:]).astype(jnp.bfloat16)
    mixed = lax.psum_scatter(
        jnp.dot(hidden, down_weight, preferred_element_type=jnp.float32),
        "loop",
        scatter_dimension=0,
        tiled=True,
    )
    return mixed.astype(jnp.bfloat16)


def solution(mesh):
    return jax.shard_map(
        shards,
        mesh=mesh,
        in_specs=(
            P("loop", "narrow"),
            P("narrow", "loop"),
            P("narrow", "loop"),
            P("loop", "narrow"),
        ),
        out_specs=P("loop", "narrow"),
        check_vma=False,
    )
```

profile of v0, /device:TPU:8, one launch (start us, length us, event | category | flops | bytes accessed | tf_op | source)
XLA Modules:
  0.0 507.0 jit_solution(5028401805543478411)
XLA Ops:
  6.5 0.0 copy-start
  6.5 0.0 all-gather.2.cloned.1.call-start
  6.5 0.7 all-gather.2.cloned.1.call-update
  7.3 0.0 copy-start.2
  7.3 0.0 all-reduce.2.cloned.1.call-start
  7.3 151.5 %all-gather.2.cloned.1.call-done = bf16[1024,1024]{1,0:T(8,128)(2,1)} async-done(((bf16[16,1024]{1,0:T(8,128)(2,1)}), bf16[1024,1024]{1,0:T(8,128)(2,1)}) %all-gather.2.cloned.1.call-update) | async-done | bytes 2097168 | tf_op jit(solution)/shard_map/all_gather | solution.py:9
  158.8 0.0 copy-start.1
  158.8 3.1 fusion.6
  162.0 0.0 copy-done.2
  162.0 0.0 copy-done.1
  162.0 1.2 fusion.5
  163.1 2.3 pad_maximum_fusion
  165.4 0.0 all-reduce.2.cloned.1.call-update
  165.4 0.0 reduce-scatter.2.cloned.1.call-start
  165.5 104.9 %all-reduce.2.cloned.1.call-done = f32[1024,896]{0,1:T(8,128)} async-done(((f32[1024,896]{0,1:T(8,128)}), f32[1024,896]{0,1:T(8,128)}) %all-reduce.2.cloned.1.call-update) | async-done | bytes 3670032 | tf_op jit(solution)/shard_map/psum | solution.py:17
  270.4 0.0 copy-done
  270.4 5.3 %fusion.1 = f32[1024,1024]{1,0:T(8,128)} fusion(bf16[448,1024]{1,0:T(8,128)(2,1)S(1)} %copy-done, f32[1024,896]{0,1:T(8,128)} %all-reduce.2.cloned.1.call-done), kind=kOutput, calls=%fused_computation.3 | convolution fusion | flops 942276608 | bytes 8781824 | tf_op jit(solution)/shard_map/dot_general | solution.py:20
  275.7 0.0 reduce-scatter.2.cloned.1.call-update
  275.8 223.2 %reduce-scatter.2.cloned.1.call-done = f32[16,1024]{1,0:T(8,128)} async-done(((f32[1024,1024]{1,0:T(8,128)}), f32[16,1024]{1,0:T(8,128)}) %reduce-scatter.2.cloned.1.call-update) | async-done | bytes 65552 | tf_op jit(solution)/shard_map/reduce_scatter | solution.py:19
  499.0 1.5 convert_element_type.7
Async XLA Ops:
  6.5 263.9 %copy-start = (bf16[448,1024]{1,0:T(8,128)(2,1)S(1)}, bf16[448,1024]{1,0:T(8,128)(2,1)}, u32[]{:S(2)}) copy-start(bf16[448,1024]{1,0:T(8,128)(2,1)} %param.7) | copy-start | bytes 2752516
  6.5 152.3 %all-gather.2.cloned.1.call-start = ((), (), s32[]{:S(2)}) async-start(), calls=%async_computation.1 | async-start | bytes 2129920 | tf_op jit(solution)/shard_map/all_gather | solution.py:9
  7.3 154.7 %copy-start.2 = (bf16[1024,448]{0,1:T(8,128)(2,1)S(1)}, bf16[1024,448]{0,1:T(8,128)(2,1)}, u32[]{:S(2)}) copy-start(bf16[1024,448]{0,1:T(8,128)(2,1)} %param.5) | copy-start | bytes 2752516
  7.3 263.1 %all-reduce.2.cloned.1.call-start = ((), (), s32[]{:S(2)}) async-start(), calls=%async_computation.2 | async-start | bytes 7340032 | tf_op jit(solution)/shard_map/psum | solution.py:17
  158.8 3.1 copy-start.1
  165.4 333.5 %reduce-scatter.2.cloned.1.call-start = ((), (), s32[]{:S(2)}) async-start(), calls=%async_computation.3 | async-start | bytes 4259840 | tf_op jit(solution)/shard_map/reduce_scatter | solution.py:19
Sparse Core Ops, SparseCore 0:
  10.7 148.1 all-gather.1
  165.6 104.7 all-reduce.1
  275.9 223.0 reduce-scatter.1
where the time goes:
time: 507 us
  waiting for transfers between devices  480 us (95%)
  between operations  13.1 us (3%)
  matrix products  9.59 us (2%)
    reduce_scatter x1, waiting for transfers between devices, shards(): lax.psum_scatter(jnp.dot(hidden, down_weight, preferred_element_type=jnp....  223 us
    all_gather x1, waiting for transfers between devices, shards(): block_rows = lax.all_gather(tokens, 'loop', axis=0, tiled=True)  152 us
    psum x1, waiting for transfers between devices, shards(): totals = lax.psum(partial_sums, 'narrow')  105 us
  transfers between devices with their start and end apart: 3, of which 3 were waited for; matrix products, arithmetic and copies ran while one was open for 0% of the time, Pallas kernels for 0%

commit v1 on v0

v1 whole, which is shorter than its diff:
```python
import jax
import jax.numpy as jnp
from jax import lax
from jax.sharding import Mesh, PartitionSpec as P

AXES = ("zh", "zl", "xh", "core", "xl", "y")
Z = ("zh", "zl")
NARROW = ("xl", "y")
SWAP = [(0, 1), (1, 0)]


def f32dot(a, b):
    return jnp.dot(a, b, preferred_element_type=jnp.float32)


def shards(tokens, gate_weight, up_weight, down_weight):
    gate_other = lax.ppermute(gate_weight, "core", SWAP)
    up_other = lax.ppermute(up_weight, "core", SWAP)
    down_other = lax.ppermute(down_weight, "core", SWAP)

    rows = lax.all_gather(tokens, Z, axis=0, tiled=True)
    near = lax.all_to_all(jnp.broadcast_to(rows, (2, *rows.shape)), "xh", 0, 0)
    rows = near.reshape(-1, tokens.shape[1])
    n_rows = rows.shape[0]

    gates = jnp.concatenate((gate_weight, gate_other), axis=1)
    ups = jnp.concatenate((up_weight, up_other), axis=1)
    width = gates.shape[1]
    partial = jnp.concatenate(
        (f32dot(rows, gates).astype(jnp.bfloat16), f32dot(rows, ups).astype(jnp.bfloat16)), axis=1
    )
    partial = partial.reshape(8, n_rows // 8, 2 * width)
    parts = lax.all_to_all(partial, NARROW, 0, 0)
    totals = jnp.sum(parts.astype(jnp.float32), axis=0)
    hidden = (jax.nn.silu(totals[:, :width]) * totals[:, width:]).astype(jnp.bfloat16)
    hidden = lax.all_to_all(jnp.broadcast_to(hidden, (8, *hidden.shape)), NARROW, 0, 0)
    hidden = hidden.reshape(n_rows, width)

    downs = jnp.concatenate((down_weight, down_other), axis=0)
    mixed = f32dot(hidden, downs).astype(jnp.bfloat16)
    mixed = mixed.reshape(2, 4, 4, 16, -1)
    mixed = mixed.transpose(2, 0, 1, 3, 4).reshape(8, 64, -1)
    mixed = lax.all_to_all(mixed, ("zl", "xh"), 0, 0)
    mixed = jnp.sum(mixed.astype(jnp.float32), axis=0).astype(jnp.bfloat16)
    mixed = lax.all_to_all(mixed.reshape(4, 16, -1), "zh", 0, 0)
    return jnp.sum(mixed.astype(jnp.float32), axis=0).astype(jnp.bfloat16)


def solution(mesh):
    fine = Mesh(mesh.devices.reshape(4, 4, 2, 2, 2, 4), AXES)
    loop, narrow = ("zh", "zl", "xh", "core"), NARROW
    return jax.shard_map(
        shards,
        mesh=fine,
        in_specs=(P(loop, narrow), P(narrow, loop), P(narrow, loop), P(loop, narrow)),
        out_specs=P(loop, narrow),
        check_vma=False,
    )
```

time: 507 us -> 148 us (0.29)
  the two profiles are of different devices: /device:TPU:8 before, /device:TPU:2 now
where the time goes in v1:
time: 148 us
  blocking collectives  99.5 us (67%)
  waiting for transfers between devices  21.9 us (15%)
  starting transfers between devices  16.6 us (11%)
  matrix products  4.72 us (3%)
  local copies, waits for them, and re-layouts  3.77 us (3%)
    all_gather x1, blocking collectives, shards(): rows = lax.all_gather(tokens, Z, axis=0, tiled=True)  38.8 us
    all_to_all x1, blocking collectives, shards(): mixed = lax.all_to_all(mixed, ('zl', 'xh'), 0, 0)  23.7 us
    all_to_all x1, blocking collectives, shards(): mixed = lax.all_to_all(mixed.reshape(4, 16, -1), 'zh', 0, 0)  22.8 us
    all_to_all x1, blocking collectives, shards(): near = lax.all_to_all(jnp.broadcast_to(rows, (2, *rows.shape)), 'xh', 0, 0)  14.2 us
    all_to_all x1, waiting for transfers between devices, shards(): parts = lax.all_to_all(partial, NARROW, 0, 0)  12.6 us
    all_to_all x1, waiting for transfers between devices, shards(): lax.all_to_all(jnp.broadcast_to(hidden, (8, *hidden.shape)), NARROW, 0, 0)  9.33 us
    all_to_all x1, starting transfers between devices, shards(): parts = lax.all_to_all(partial, NARROW, 0, 0)  6.06 us
    dot_general x3, matrix products, f32dot(): return jnp.dot(a, b, preferred_element_type=jnp.float32)  4.72 us
  transfers between devices with their start and end apart: 5, of which 2 were waited for; matrix products, arithmetic and copies ran while one was open for 2% of the time, Pallas kernels for 0%

profile of v1, /device:TPU:2, one launch (start us, length us, event | category | flops | bytes accessed | tf_op | source)
XLA Modules:
  0.0 147.9 jit_solution(17875800447940083722)
XLA Ops:
  0.0 1.9 %collective-permute-start = (bf16[1024,448]{0,1:T(8,128)(2,1)}, bf16[1024,448]{0,1:T(8,128)(2,1)S(1)}, u32[]{:S(2)}, u32[]{:S(2)}) collective-permute-start(bf16[1024,448]{0,1:T(8,128)(2,1)} %param.5), channel_id=1, source_target_pairs={{0,8},{8,0},{1,9},{9,1},{2,10},{10,2},{3,11},{11,3},{4,12},{12,4},... | collective-permute-start | bytes 2752520 | tf_op jit(solution)/shard_map/ppermute | solution.py:17
  1.9 2.4 %collective-permute-start.1 = (bf16[1024,448]{0,1:T(8,128)(2,1)}, bf16[1024,448]{0,1:T(8,128)(2,1)S(1)}, u32[]{:S(2)}, u32[]{:S(2)}) collective-permute-start(bf16[1024,448]{0,1:T(8,128)(2,1)} %param.6), channel_id=1, source_target_pairs={{0,8},{8,0},{1,9},{9,1},{2,10},{10,2},{3,11},{11,3},{4,12},{12,4},... | collective-permute-start | bytes 2752520 | tf_op jit(solution)/shard_map/ppermute | solution.py:18
  4.3 38.8 %all_gather.3 = bf16[256,1024]{1,0:T(8,128)(2,1)S(1)} all-gather(bf16[16,1024]{1,0:T(8,128)(2,1)} %param.4), channel_id=1, replica_groups=mesh['zh'=4,'zl'=4,'xh'=2,'core'=2,'xl'=2,'y'=4] {'zh','zl'}, dimensions={0}, use_global_device_ids=true | all-gather | bytes 557056 | tf_op jit(solution)/shard_map/all_gather | solution.py:21
  43.2 0.0 copy-start
  43.2 0.1 broadcast_in_dim.6
  43.3 14.2 %all_to_all.25 = bf16[2,256,1024]{2,1,0:T(8,128)(2,1)S(1)} all-to-all(bf16[2,256,1024]{2,1,0:T(8,128)(2,1)S(1)} %broadcast_in_dim.6), channel_id=1, replica_groups=mesh['zh'=4,'zl'=4,'xh'=2,'core'=2,'xl'=2,'y'=4] {'xh'}, dimensions={0} | all-to-all | bytes 2097152 | tf_op jit(solution)/shard_map/all_to_all | solution.py:22
  57.5 0.0 collective-permute-done
  57.5 0.0 copy-done
  57.5 0.0 copy-start.1
  57.5 1.1 fusion.21
  58.7 0.0 collective-permute-done.1
  58.7 0.0 copy-done.1
  58.7 1.1 fusion.24
  59.8 0.1 pad_maximum_fusion
  60.0 2.5 %copy.7 = bf16[512,1792]{1,0:T(8,128)(2,1)} copy(bf16[512,1792]{0,1:T(8,128)(2,1)S(1)} %pad_maximum_fusion) | data formatting | bytes 3670016 | tf_op jit(solution)/shard_map/concatenate | solution.py:29
  62.4 0.0 copy-start.2
  62.4 6.1 %all-to-all-start.1 = ((bf16[8,64,1792]{2,1,0:T(8,128)(2,1)}), bf16[8,64,1792]{2,1,0:T(8,128)(2,1)S(1)}, u32[]{:S(2)}, u32[]{:S(2)}) async-start(bf16[8,64,1792]{2,1,0:T(8,128)(2,1)} %bitcast.3), calls=%async_computation.1 | async-start | bytes 3670016 | tf_op jit(solution)/shard_map/all_to_all | solution.py:33
  68.5 0.0 copy-done.2
  68.5 1.9 %collective-permute-start.2 = (bf16[448,1024]{1,0:T(8,128)(2,1)S(1)}, bf16[448,1024]{1,0:T(8,128)(2,1)}, u32[]{:S(2)}, u32[]{:S(2)}) collective-permute-start(bf16[448,1024]{1,0:T(8,128)(2,1)S(1)} %copy-done.2), channel_id=1, source_target_pairs={{0,8},{8,0},{1,9},{9,1},{2,10},{10,2},{3,11},{11,3},{4,12},{12,4},... | collective-permute-start | bytes 2752520 | tf_op jit(solution)/shard_map/ppermute | solution.py:19
  70.4 12.6 %all-to-all-done.1 = bf16[8,64,1792]{2,1,0:T(8,128)(2,1)S(1)} async-done(((bf16[8,64,1792]{2,1,0:T(8,128)(2,1)}), bf16[8,64,1792]{2,1,0:T(8,128)(2,1)S(1)}, u32[]{:S(2)}, u32[]{:S(2)}) %all-to-all-start.1) | async-done | bytes 1835040 | tf_op jit(solution)/shard_map/all_to_all | solution.py:33
  83.0 0.2 convert_reduce_fusion
  83.3 0.1 fusion.27
  83.3 1.0 broadcast_in_dim.7
  84.4 4.3 %all-to-all-start.2 = ((bf16[8,64,896]{2,1,0:T(8,128)(2,1)}), bf16[8,64,896]{2,1,0:T(8,128)(2,1)S(1)}, u32[]{:S(2)}, u32[]{:S(2)}) async-start(bf16[8,64,896]{2,1,0:T(8,128)(2,1)} %broadcast_in_dim.7), calls=%async_computation.2 | async-start | bytes 1835008 | tf_op jit(solution)/shard_map/all_to_all | solution.py:36
  88.7 0.0 collective-permute-done.2
  88.7 9.3 %all-to-all-done.2 = bf16[8,64,896]{2,1,0:T(8,128)(2,1)S(1)} async-done(((bf16[8,64,896]{2,1,0:T(8,128)(2,1)}), bf16[8,64,896]{2,1,0:T(8,128)(2,1)S(1)}, u32[]{:S(2)}, u32[]{:S(2)}) %all-to-all-start.2) | async-done | bytes 917536 | tf_op jit(solution)/shard_map/all_to_all | solution.py:36
  98.1 2.4 %fusion.12 = bf16[512,1024]{1,0:T(8,128)(2,1)S(1)} fusion(bf16[512,896]{1,0:T(8,128)(2,1)S(1)} %bitcast.19, bf16[448,1024]{1,0:T(8,128)(2,1)} %collective-permute-done.2, bf16[448,1024]{1,0:T(8,128)(2,1)S(1)} %copy-done.2), kind=kOutput, calls=%fused_computation.14 | convolution fusion | flops 943718400 | bytes 3801088 | tf_op jit(solution)/shard_map/dot_general | solution.py:13
  100.5 0.1 copy.8
  100.6 23.7 %all_to_all.26 = bf16[8,64,1024]{2,1,0:T(8,128)(2,1)S(1)} all-to-all(bf16[8,64,1024]{2,1,0:T(8,128)(2,1)S(1)} %bitcast.15), channel_id=1, replica_groups=mesh['zh'=4,'zl'=4,'xh'=2,'core'=2,'xl'=2,'y'=4] {'zl','xh'}, dimensions={0} | all-to-all | bytes 2097152 | tf_op jit(solution)/shard_map/all_to_all | solution.py:43
  124.3 0.2 reduce_sum.34
  124.5 22.8 %all_to_all.27 = bf16[4,16,1024]{2,1,0:T(8,128)(2,1)S(1)} all-to-all(bf16[4,16,1024]{2,1,0:T(8,128)(2,1)S(1)} %bitcast.20), channel_id=1, replica_groups=mesh['zh'=4,'zl'=4,'xh'=2,'core'=2,'xl'=2,'y'=4] {'zh'}, dimensions={0} | all-to-all | bytes 262144 | tf_op jit(solution)/shard_map/all_to_all | solution.py:45
  147.3 0.6 reduce_sum.35
Async XLA Ops:
  0.0 57.5 %collective-permute-start = (bf16[1024,448]{0,1:T(8,128)(2,1)}, bf16[1024,448]{0,1:T(8,128)(2,1)S(1)}, u32[]{:S(2)}, u32[]{:S(2)}) collective-permute-start(bf16[1024,448]{0,1:T(8,128)(2,1)} %param.5), channel_id=1, source_target_pairs={{0,8},{8,0},{1,9},{9,1},{2,10},{10,2},{3,11},{11,3},{4,12},{12,4},... | collective-permute-start | bytes 2752520 | tf_op jit(solution)/shard_map/ppermute | solution.py:17
  1.9 56.8 %collective-permute-start.1 = (bf16[1024,448]{0,1:T(8,128)(2,1)}, bf16[1024,448]{0,1:T(8,128)(2,1)S(1)}, u32[]{:S(2)}, u32[]{:S(2)}) collective-permute-start(bf16[1024,448]{0,1:T(8,128)(2,1)} %param.6), channel_id=1, source_target_pairs={{0,8},{8,0},{1,9},{9,1},{2,10},{10,2},{3,11},{11,3},{4,12},{12,4},... | collective-permute-start | bytes 2752520 | tf_op jit(solution)/shard_map/ppermute | solution.py:18
  43.2 14.4 %copy-start = (bf16[1024,448]{0,1:T(8,128)(2,1)S(1)}, bf16[1024,448]{0,1:T(8,128)(2,1)}, u32[]{:S(2)}) copy-start(bf16[1024,448]{0,1:T(8,128)(2,1)} %param.5) | copy-start | bytes 2752516
  57.5 1.2 copy-start.1
  62.4 6.1 %copy-start.2 = (bf16[448,1024]{1,0:T(8,128)(2,1)S(1)}, bf16[448,1024]{1,0:T(8,128)(2,1)}, u32[]{:S(2)}) copy-start(bf16[448,1024]{1,0:T(8,128)(2,1)} %param.7) | copy-start | bytes 2752516
  62.4 20.6 %all-to-all-start.1 = ((bf16[8,64,1792]{2,1,0:T(8,128)(2,1)}), bf16[8,64,1792]{2,1,0:T(8,128)(2,1)S(1)}, u32[]{:S(2)}, u32[]{:S(2)}) async-start(bf16[8,64,1792]{2,1,0:T(8,128)(2,1)} %bitcast.3), calls=%async_computation.1 | async-start | bytes 3670016 | tf_op jit(solution)/shard_map/all_to_all | solution.py:33
  68.5 20.2 %collective-permute-start.2 = (bf16[448,1024]{1,0:T(8,128)(2,1)S(1)}, bf16[448,1024]{1,0:T(8,128)(2,1)}, u32[]{:S(2)}, u32[]{:S(2)}) collective-permute-start(bf16[448,1024]{1,0:T(8,128)(2,1)S(1)} %copy-done.2), channel_id=1, source_target_pairs={{0,8},{8,0},{1,9},{9,1},{2,10},{10,2},{3,11},{11,3},{4,12},{12,4},... | collective-permute-start | bytes 2752520 | tf_op jit(solution)/shard_map/ppermute | solution.py:19
  84.4 13.7 %all-to-all-start.2 = ((bf16[8,64,896]{2,1,0:T(8,128)(2,1)}), bf16[8,64,896]{2,1,0:T(8,128)(2,1)S(1)}, u32[]{:S(2)}, u32[]{:S(2)}) async-start(bf16[8,64,896]{2,1,0:T(8,128)(2,1)} %broadcast_in_dim.7), calls=%async_computation.2 | async-start | bytes 1835008 | tf_op jit(solution)/shard_map/all_to_all | solution.py:36

commit v2 on v0

v2 whole, which is shorter than its diff:
```python
import jax
import jax.numpy as jnp
from jax import lax
from jax.experimental import pallas as pl
from jax.experimental.pallas import tpu as pltpu
from jax.sharding import Mesh, PartitionSpec as P

AXES = ("zh", "za", "zb", "xh", "core", "xl", "y")
NARROW = ("xl", "y")
SWAP = [(0, 1), (1, 0)]
VMEM = pl.BlockSpec(memory_space=pltpu.VMEM)
SMEM = pl.BlockSpec(memory_space=pltpu.SMEM)


def total(parts):
    return jnp.sum(parts.astype(jnp.float32), axis=0)


def matmul(a, b, b_dim):
    return lax.dot_general(a, b, (((1,), (b_dim,)), ((), ())), preferred_element_type=jnp.float32)


def own_kernel(x_ref, *refs):
    *weight_refs, out_ref = refs
    width = weight_refs[0].shape[0]
    for i, w_ref in enumerate(weight_refs):
        product = matmul(x_ref[...], w_ref[...], 1)
        out_ref[:, i * width : (i + 1) * width] = product.astype(out_ref.dtype)


def join_kernel(at_xh_ref, x_ref, own_ref, *refs):
    *weight_refs, out_ref = refs
    width = weight_refs[0].shape[0]
    at_xh = at_xh_ref[0]

    def put(slot, columns, block):
        for at in range(16):
            high, low, za, zb = at // 8, at // 4 % 2, at // 2 % 2, at % 2
            out_ref[za, slot, high, zb, low, :, columns] = block[at * 16 : (at + 1) * 16]

    for i, w_ref in enumerate(weight_refs):
        columns = slice(i * width, (i + 1) * width)
        put(1 - at_xh, columns, matmul(x_ref[...], w_ref[...], 1).astype(out_ref.dtype))
    put(at_xh, slice(None), own_ref[...])


def down_kernel(at_zb_ref, hidden_ref, *refs):
    *weight_refs, out_ref, joined_ref = refs
    width = weight_refs[0].shape[0]
    at_zb = at_zb_ref[0]
    for i, w_ref in enumerate(weight_refs):
        joined_ref[i // 2, i % 2 * width : (i % 2 + 1) * width] = w_ref[...]
    mixed = matmul(hidden_ref[at_zb], joined_ref[0], 0)
    mixed = mixed + matmul(hidden_ref[1 - at_zb], joined_ref[1], 0)
    out_ref[...] = mixed.astype(out_ref.dtype)


def call(kernel, specs, out_shape, flops, *args, scratch=()):
    return pl.pallas_call(
        kernel,
        out_shape=jax.ShapeDtypeStruct(out_shape, jnp.bfloat16),
        in_specs=specs,
        out_specs=VMEM,
        scratch_shapes=scratch,
        cost_estimate=pl.CostEstimate(
            flops=flops, bytes_accessed=2 * sum(a.size for a in args), transcendentals=0
        ),
        compiler_params=pltpu.CompilerParams(vmem_limit_bytes=32 << 20),
    )(*args)


def shards(tokens, gate_weight, up_weight, down_weight):
    depth = tokens.shape[1]
    at_xh = lax.axis_index("xh").reshape(1)
    at_zb = lax.axis_index("zb").reshape(1)
    gate, up = gate_weight.T, up_weight.T
    width = gate.shape[0]
    weights = [gate, lax.ppermute(gate, "core", SWAP), up, lax.ppermute(up, "core", SWAP)]

    rows = lax.all_gather(tokens, ("zh", "za", "zb"), axis=0, tiled=True)
    n_rows = rows.shape[0]
    other_rows = lax.ppermute(rows, "xh", SWAP)
    flops = 8 * n_rows * depth * width
    own = call(own_kernel, [VMEM] * 5, (n_rows, 4 * width), flops, rows, *weights)
    partial = call(
        join_kernel,
        [SMEM] + [VMEM] * 6,
        (2, 2, 2, 2, 2, 16, 4 * width),
        flops,
        at_xh,
        other_rows,
        own,
        *weights,
    )
    down_weight, partial = lax.optimization_barrier((down_weight, partial))
    down_far = lax.ppermute(down_weight, "zb", SWAP)
    parts = lax.all_to_all(partial.reshape(8, 2, 32, 4 * width), NARROW, 0, 0)
    parts, down_weight, down_far = lax.optimization_barrier((parts, down_weight, down_far))
    downs = [down_weight, lax.ppermute(down_weight, "core", SWAP)]
    downs += [down_far, lax.ppermute(down_far, "core", SWAP)]

    totals = total(parts)
    hidden = (jax.nn.silu(totals[..., : 2 * width]) * totals[..., 2 * width :]).astype(jnp.bfloat16)
    hidden = jnp.broadcast_to(hidden[:, None], (2, 8, 32, 2 * width)).reshape(16, 32, 2 * width)
    hidden = lax.all_to_all(hidden, ("zb", *NARROW), 0, 0).reshape(2, n_rows, 2 * width)
    mixed = call(
        down_kernel,
        [SMEM] + [VMEM] * 5,
        (n_rows, depth),
        8 * n_rows * depth * width,
        at_zb,
        hidden,
        *downs,
        scratch=[pltpu.VMEM((2, 2 * width, depth), jnp.bfloat16)],
    )
    mixed = total(lax.all_to_all(mixed.reshape(4, 64, depth), ("za", "xh"), 0, 0))
    mixed = lax.all_to_all(mixed.astype(jnp.bfloat16).reshape(4, 16, depth), "zh", 0, 0)
    return total(mixed).astype(jnp.bfloat16)


def solution(mesh):
    fine = Mesh(mesh.devices.reshape(4, 2, 2, 2, 2, 2, 4), AXES)
    loop = ("zh", "za", "zb", "xh", "core")
    return jax.shard_map(
        shards,
        mesh=fine,
        in_specs=(P(loop, NARROW), P(NARROW, loop), P(NARROW, loop), P(loop, NARROW)),
        out_specs=P(loop, NARROW),
        check_vma=False,
    )
```

time: 507 us -> 140 us (0.28)
  waiting for transfers between devices: 480 us -> 23.8 us
  blocking collectives: 0 us -> 75.8 us
  starting transfers between devices: 0.08 us -> 27.2 us
  between operations: 13.1 us -> 0.12 us
  matrix products: 9.59 us -> 0 us
  Pallas kernels: 0 us -> 6.69 us
    reduce_scatter x1 -> x0, waiting for transfers between devices: 223 us -> none  [shards(): lax.psum_scatter(jnp.dot(hidden, down_weight, preferred_element_type=jnp....]
    all_gather x1 -> x0, waiting for transfers between devices: 152 us -> none  [shards(): block_rows = lax.all_gather(tokens, 'loop', axis=0, tiled=True)]
    psum x1 -> x0, waiting for transfers between devices: 105 us -> none  [shards(): totals = lax.psum(partial_sums, 'narrow')]
    all_gather x0 -> x1, blocking collectives: none -> 38.8 us  [shards(): rows = lax.all_gather(tokens, ('zh', 'za', 'zb'), axis=0, tiled=True)]
    all_to_all x0 -> x2, blocking collectives: none -> 37 us  [the longest x1 20.2 us: shards(): lax.all_to_all(mixed.astype(jnp.bfloat16).reshape(4, 16, depth), 'zh', 0, 0)]
    ppermute x0 -> x6, waiting for transfers between devices: none -> 19.7 us  [the longest x1 13.6 us: shards(): down_far = lax.ppermute(down_weight, 'zb', SWAP)]
    ppermute x0 -> x6, starting transfers between devices: none -> 15.5 us  [the longest x1 4.92 us: shards(): other_rows = lax.ppermute(rows, 'xh', SWAP)]
    all_to_all x0 -> x2, starting transfers between devices: none -> 11.7 us  [the longest x1 5.97 us: shards(): parts = lax.all_to_all(partial.reshape(8, 2, 32, 4 * width), NARROW, 0, 0)]
  transfers between devices with their start and end apart: 3 -> 8, of which waited for: 3 -> 5; matrix products, arithmetic and copies ran while one was open for 0% -> 0% of each run, Pallas kernels for 0% -> 1%
where the time goes in v2:
time: 140 us
  blocking collectives  75.8 us (54%)
  starting transfers between devices  27.2 us (19%)
  waiting for transfers between devices  23.8 us (17%)
  Pallas kernels  6.69 us (5%)
  local copies, waits for them, and re-layouts  3.39 us (2%)
  other arithmetic  2.6 us (2%)
    all_gather x1, blocking collectives, shards(): rows = lax.all_gather(tokens, ('zh', 'za', 'zb'), axis=0, tiled=True)  38.8 us
    all_to_all x1, blocking collectives, shards(): lax.all_to_all(mixed.astype(jnp.bfloat16).reshape(4, 16, depth), 'zh', 0, 0)  20.2 us
    all_to_all x1, blocking collectives, shards(): lax.all_to_all(mixed.reshape(4, 64, depth), ('za', 'xh'), 0, 0)  16.8 us
    ppermute x1, waiting for transfers between devices, shards(): down_far = lax.ppermute(down_weight, 'zb', SWAP)  13.6 us
    pallas_call x3, Pallas kernels, call(): pl.pallas_call(kernel, out_shape=jax.ShapeDtypeStruct(out_shape, jnp.bflo...  6.69 us
    all_to_all x1, starting transfers between devices, shards(): parts = lax.all_to_all(partial.reshape(8, 2, 32, 4 * width), NARROW, 0, 0)  5.97 us
    all_to_all x1, starting transfers between devices, shards(): lax.all_to_all(hidden, ('zb', *NARROW), 0, 0).reshape(2, n_rows, 2 * width)  5.72 us
    ppermute x1, starting transfers between devices, shards(): other_rows = lax.ppermute(rows, 'xh', SWAP)  4.92 us
  transfers between devices with their start and end apart: 8, of which 5 were waited for; matrix products, arithmetic and copies ran while one was open for 0% of the time, Pallas kernels for 1%

profile of v2, /device:TPU:8, one launch (start us, length us, event | category | flops | bytes accessed | tf_op | source)
XLA Modules:
  0.0 139.6 jit_solution(8454547733709216298)
XLA Ops:
  0.0 1.9 %collective-permute-start.1 = (bf16[448,1024]{1,0:T(8,128)(2,1)}, bf16[448,1024]{1,0:T(8,128)(2,1)S(1)}, u32[]{:S(2)}, u32[]{:S(2)}) collective-permute-start(bf16[448,1024]{1,0:T(8,128)(2,1)} %bitcast.9), channel_id=1, source_target_pairs={{0,8},{8,0},{1,9},{9,1},{2,10},{10,2},{3,11},{11,3},{4,12},{12,4},... | collective-permute-start | bytes 2752520 | tf_op jit(solution)/shard_map/ppermute | solution.py:78
  1.9 2.4 %collective-permute-start.2 = (bf16[448,1024]{1,0:T(8,128)(2,1)}, bf16[448,1024]{1,0:T(8,128)(2,1)S(1)}, u32[]{:S(2)}, u32[]{:S(2)}) collective-permute-start(bf16[448,1024]{1,0:T(8,128)(2,1)} %bitcast.12), channel_id=1, source_target_pairs={{0,8},{8,0},{1,9},{9,1},{2,10},{10,2},{3,11},{11,3},{4,12},{12,4},... | collective-permute-start | bytes 2752520 | tf_op jit(solution)/shard_map/ppermute | solution.py:78
  4.3 38.8 %all_gather.3.x_ref = bf16[256,1024]{1,0:T(8,128)(2,1)S(1)} all-gather(bf16[16,1024]{1,0:T(8,128)(2,1)} %param.4), channel_id=1, replica_groups=mesh['zh'=4,'za'=2,'zb'=2,'xh'=2,'core'=2,'xl'=2,'y'=4] {'zh','za','zb'}, dimensions={0}, use_global_device_ids=true | all-gather | bytes 557056 | tf_op jit(solution)/shard_map/all_gather | solution.py:80
  43.2 4.9 %collective-permute-start = (bf16[256,1024]{1,0:T(8,128)(2,1)S(1)}, bf16[256,1024]{1,0:T(8,128)(2,1)S(1)}, u32[]{:S(2)}, u32[]{:S(2)}) collective-permute-start(bf16[256,1024]{1,0:T(8,128)(2,1)S(1)} %all_gather.3.x_ref), channel_id=1, source_target_pairs={{0,16},{16,0},{1,17},{17,1},{2,18},{18,2},{3,19},{19,3},{4,20},{20... | collective-permute-start | bytes 1572872 | tf_op jit(solution)/shard_map/ppermute | solution.py:82
  48.1 0.0 collective-permute-done.1.refs_1_
  48.1 0.0 collective-permute-done.2.refs_3_
  48.1 0.0 copy-start
  48.1 1.2 copy-done
  49.3 0.0 copy-start.2
  49.3 1.2 copy-done.2
  50.5 0.0 copy-start.1
  50.5 0.0 copy-start.3
  50.5 1.3 shard_map.46.own_ref
  51.8 3.9 %collective-permute-done.x_ref = bf16[256,1024]{1,0:T(8,128)(2,1)S(1)} collective-permute-done((bf16[256,1024]{1,0:T(8,128)(2,1)S(1)}, bf16[256,1024]{1,0:T(8,128)(2,1)S(1)}, u32[]{:S(2)}, u32[]{:S(2)}) %collective-permute-start) | collective-permute-done | bytes 524320 | tf_op jit(solution)/shard_map/ppermute | solution.py:82
  55.7 0.0 copy-done.1
  55.7 0.0 copy-done.3
  55.7 2.7 %shard_map.47 = bf16[2,2,2,2,2,16,1792]{6,5,4,3,2,1,0:T(8,128)(2,1)} custom-call(s32[1]{0:T(128)} %bitcast.1.at_xh_ref, bf16[256,1024]{1,0:T(8,128)(2,1)S(1)} %collective-permute-done.x_ref, bf16[256,1792]{1,0:T(8,128)(2,1)S(1)} %shard_map.46.own_ref, bf16[448,1024]{1,0:T(8,128)(2,1)S(1)} %bitcast.11, bf16[448,1024]{1,0:T(8,128)(2,1)S(1)} %collective-permute-done.1.refs_1_, ...), custom_call_target="tpu_custom_call" | custom-call | flops 939524096 | bytes 5111810 | tf_op jit(solution)/shard_map/pallas_call | solution.py:59
  58.4 0.0 copy-start.4
  58.4 6.0 %all-to-all-start = ((bf16[8,2,32,1792]{3,2,1,0:T(8,128)(2,1)}), bf16[8,2,32,1792]{3,2,1,0:T(8,128)(2,1)}, u32[]{:S(2)}, u32[]{:S(2)}) async-start(bf16[8,2,32,1792]{3,2,1,0:T(8,128)(2,1)} %bitcast.4), calls=%async_computation | async-start | bytes 3670016 | tf_op jit(solution)/shard_map/all_to_all | solution.py:97
  64.4 0.0 copy-done.4
  64.4 1.9 %collective-permute-start.3 = (bf16[448,1024]{1,0:T(8,128)(2,1)S(1)}, bf16[448,1024]{1,0:T(8,128)(2,1)S(1)}, u32[]{:S(2)}, u32[]{:S(2)}) collective-permute-start(bf16[448,1024]{1,0:T(8,128)(2,1)S(1)} %copy-done.4), channel_id=1, source_target_pairs={{0,32},{32,0},{1,33},{33,1},{2,34},{34,2},{3,35},{35,3},{4,36},{36... | collective-permute-start | bytes 2752520 | tf_op jit(solution)/shard_map/ppermute | solution.py:96
  66.3 13.6 %collective-permute-done.3.refs_2_ = bf16[448,1024]{1,0:T(8,128)(2,1)S(1)} collective-permute-done((bf16[448,1024]{1,0:T(8,128)(2,1)S(1)}, bf16[448,1024]{1,0:T(8,128)(2,1)S(1)}, u32[]{:S(2)}, u32[]{:S(2)}) %collective-permute-start.3) | collective-permute-done | bytes 917536 | tf_op jit(solution)/shard_map/ppermute | solution.py:96
  79.9 0.0 all-to-all-done
  79.9 1.8 %convert_reduce_fusion = f32[2,32,1792]{2,1,0:T(8,128)S(1)} fusion(bf16[8,2,32,1792]{3,2,1,0:T(8,128)(2,1)} %all-to-all-done), kind=kLoop, calls=%fused_computation | loop fusion | flops 1720320 | bytes 2293760 | tf_op jit(solution)/shard_map/reduce_sum | solution.py:16
  81.7 0.1 fusion
  81.8 1.0 broadcast_in_dim.2
  82.8 5.7 %all-to-all-start.1 = ((bf16[16,32,896]{2,1,0:T(8,128)(2,1)}), bf16[16,32,896]{2,1,0:T(8,128)(2,1)S(1)}, u32[]{:S(2)}, u32[]{:S(2)}) async-start(bf16[16,32,896]{2,1,0:T(8,128)(2,1)} %bitcast.17), calls=%async_computation.1 | async-start | bytes 1835008 | tf_op jit(solution)/shard_map/all_to_all | solution.py:105
  88.5 1.9 %collective-permute-start.4 = (bf16[448,1024]{1,0:T(8,128)(2,1)S(1)}, bf16[448,1024]{1,0:T(8,128)(2,1)}, u32[]{:S(2)}, u32[]{:S(2)}) collective-permute-start(bf16[448,1024]{1,0:T(8,128)(2,1)S(1)} %copy-done.4), channel_id=1, source_target_pairs={{0,8},{8,0},{1,9},{9,1},{2,10},{10,2},{3,11},{11,3},{4,12},{12,4},... | collective-permute-start | bytes 2752520 | tf_op jit(solution)/shard_map/ppermute | solution.py:99
  90.5 2.4 %collective-permute-start.5 = (bf16[448,1024]{1,0:T(8,128)(2,1)S(1)}, bf16[448,1024]{1,0:T(8,128)(2,1)}, u32[]{:S(2)}, u32[]{:S(2)}) collective-permute-start(bf16[448,1024]{1,0:T(8,128)(2,1)S(1)} %collective-permute-done.3.refs_2_), channel_id=1, source_target_pairs={{0,8},{8,0},{1,9},{9,1},{2,10},{10,2},{3,11},{11,3},{4,12},{12,4},... | collective-permute-start | bytes 2752520 | tf_op jit(solution)/shard_map/ppermute | solution.py:100
  92.9 0.2 collective-permute-done.4.refs_1_
  93.0 2.1 %collective-permute-done.5.refs_3_ = bf16[448,1024]{1,0:T(8,128)(2,1)} collective-permute-done((bf16[448,1024]{1,0:T(8,128)(2,1)S(1)}, bf16[448,1024]{1,0:T(8,128)(2,1)}, u32[]{:S(2)}, u32[]{:S(2)}) %collective-permute-start.5) | collective-permute-done | bytes 917536 | tf_op jit(solution)/shard_map/ppermute | solution.py:100
  95.1 4.0 %all-to-all-done.1 = bf16[16,32,896]{2,1,0:T(8,128)(2,1)S(1)} async-done(((bf16[16,32,896]{2,1,0:T(8,128)(2,1)}), bf16[16,32,896]{2,1,0:T(8,128)(2,1)S(1)}, u32[]{:S(2)}, u32[]{:S(2)}) %all-to-all-start.1) | async-done | bytes 917536 | tf_op jit(solution)/shard_map/all_to_all | solution.py:105
  99.1 2.7 %shard_map.48 = bf16[256,1024]{1,0:T(8,128)(2,1)S(1)} custom-call(s32[1]{0:T(128)} %bitcast.at_zb_ref, bf16[2,256,896]{2,1,0:T(8,128)(2,1)S(1)} %bitcast.15, bf16[448,1024]{1,0:T(8,128)(2,1)S(1)} %copy-done.4, bf16[448,1024]{1,0:T(8,128)(2,1)} %collective-permute-done.4.refs_1_, bf16[448,1024]{1,0:T(8,128)(2,1)S(1)} %collective-permute-done.3.refs_2_, ...), custom_call_target="tpu_custom_call" | custom-call | flops 939524096 | bytes 4587522 | tf_op jit(solution)/shard_map/pallas_call | solution.py:59
  101.8 16.8 %all_to_all.20 = bf16[4,64,1024]{2,1,0:T(8,128)(2,1)S(1)} all-to-all(bf16[4,64,1024]{2,1,0:T(8,128)(2,1)S(1)} %bitcast.16), channel_id=1, replica_groups=mesh['zh'=4,'za'=2,'zb'=2,'xh'=2,'core'=2,'xl'=2,'y'=4] {'za','xh'}, dimensions={0} | all-to-all | bytes 1048576 | tf_op jit(solution)/shard_map/all_to_all | solution.py:116
  118.7 0.1 reduce_sum.34
  118.8 20.2 %all_to_all.21 = bf16[4,16,1024]{2,1,0:T(8,128)(2,1)S(1)} all-to-all(bf16[4,16,1024]{2,1,0:T(8,128)(2,1)S(1)} %bitcast.18), channel_id=1, replica_groups=mesh['zh'=4,'za'=2,'zb'=2,'xh'=2,'core'=2,'xl'=2,'y'=4] {'zh'}, dimensions={0} | all-to-all | bytes 262144 | tf_op jit(solution)/shard_map/all_to_all | solution.py:117
  138.9 0.6 reduce_sum.35
Async XLA Ops:
  0.0 48.1 %collective-permute-start.1 = (bf16[448,1024]{1,0:T(8,128)(2,1)}, bf16[448,1024]{1,0:T(8,128)(2,1)S(1)}, u32[]{:S(2)}, u32[]{:S(2)}) collective-permute-start(bf16[448,1024]{1,0:T(8,128)(2,1)} %bitcast.9), channel_id=1, source_target_pairs={{0,8},{8,0},{1,9},{9,1},{2,10},{10,2},{3,11},{11,3},{4,12},{12,4},... | collective-permute-start | bytes 2752520 | tf_op jit(solution)/shard_map/ppermute | solution.py:78
  1.9 46.2 %collective-permute-start.2 = (bf16[448,1024]{1,0:T(8,128)(2,1)}, bf16[448,1024]{1,0:T(8,128)(2,1)S(1)}, u32[]{:S(2)}, u32[]{:S(2)}) collective-permute-start(bf16[448,1024]{1,0:T(8,128)(2,1)} %bitcast.12), channel_id=1, source_target_pairs={{0,8},{8,0},{1,9},{9,1},{2,10},{10,2},{3,11},{11,3},{4,12},{12,4},... | collective-permute-start | bytes 2752520 | tf_op jit(solution)/shard_map/ppermute | solution.py:78
  43.2 12.6 %collective-permute-start = (bf16[256,1024]{1,0:T(8,128)(2,1)S(1)}, bf16[256,1024]{1,0:T(8,128)(2,1)S(1)}, u32[]{:S(2)}, u32[]{:S(2)}) collective-permute-start(bf16[256,1024]{1,0:T(8,128)(2,1)S(1)} %all_gather.3.x_ref), channel_id=1, source_target_pairs={{0,16},{16,0},{1,17},{17,1},{2,18},{18,2},{3,19},{19,3},{4,20},{20... | collective-permute-start | bytes 1572872 | tf_op jit(solution)/shard_map/ppermute | solution.py:82
  48.1 1.2 copy-start
  49.3 1.2 copy-start.2
  50.5 5.3 %copy-start.1 = (bf16[1024,448]{0,1:T(8,128)(2,1)S(1)}, bf16[1024,448]{0,1:T(8,128)(2,1)}, u32[]{:S(2)}) copy-start(bf16[1024,448]{0,1:T(8,128)(2,1)} %param.5) | copy-start | bytes 2752516
  50.5 5.3 %copy-start.3 = (bf16[1024,448]{0,1:T(8,128)(2,1)S(1)}, bf16[1024,448]{0,1:T(8,128)(2,1)}, u32[]{:S(2)}) copy-start(bf16[1024,448]{0,1:T(8,128)(2,1)} %param.6) | copy-start | bytes 2752516
  58.4 6.0 %copy-start.4 = (bf16[448,1024]{1,0:T(8,128)(2,1)S(1)}, bf16[448,1024]{1,0:T(8,128)(2,1)}, u32[]{:S(2)}) copy-start(bf16[448,1024]{1,0:T(8,128)(2,1)} %refs_0_) | copy-start | bytes 2752516
  58.4 21.5 %all-to-all-start = ((bf16[8,2,32,1792]{3,2,1,0:T(8,128)(2,1)}), bf16[8,2,32,1792]{3,2,1,0:T(8,128)(2,1)}, u32[]{:S(2)}, u32[]{:S(2)}) async-start(bf16[8,2,32,1792]{3,2,1,0:T(8,128)(2,1)} %bitcast.4), calls=%async_computation | async-start | bytes 3670016 | tf_op jit(solution)/shard_map/all_to_all | solution.py:97
  64.4 15.5 %collective-permute-start.3 = (bf16[448,1024]{1,0:T(8,128)(2,1)S(1)}, bf16[448,1024]{1,0:T(8,128)(2,1)S(1)}, u32[]{:S(2)}, u32[]{:S(2)}) collective-permute-start(bf16[448,1024]{1,0:T(8,128)(2,1)S(1)} %copy-done.4), channel_id=1, source_target_pairs={{0,32},{32,0},{1,33},{33,1},{2,34},{34,2},{3,35},{35,3},{4,36},{36... | collective-permute-start | bytes 2752520 | tf_op jit(solution)/shard_map/ppermute | solution.py:96
  82.8 16.3 %all-to-all-start.1 = ((bf16[16,32,896]{2,1,0:T(8,128)(2,1)}), bf16[16,32,896]{2,1,0:T(8,128)(2,1)S(1)}, u32[]{:S(2)}, u32[]{:S(2)}) async-start(bf16[16,32,896]{2,1,0:T(8,128)(2,1)} %bitcast.17), calls=%async_computation.1 | async-start | bytes 1835008 | tf_op jit(solution)/shard_map/all_to_all | solution.py:105
  88.5 4.5 %collective-permute-start.4 = (bf16[448,1024]{1,0:T(8,128)(2,1)S(1)}, bf16[448,1024]{1,0:T(8,128)(2,1)}, u32[]{:S(2)}, u32[]{:S(2)}) collective-permute-start(bf16[448,1024]{1,0:T(8,128)(2,1)S(1)} %copy-done.4), channel_id=1, source_target_pairs={{0,8},{8,0},{1,9},{9,1},{2,10},{10,2},{3,11},{11,3},{4,12},{12,4},... | collective-permute-start | bytes 2752520 | tf_op jit(solution)/shard_map/ppermute | solution.py:99
  90.5 4.6 %collective-permute-start.5 = (bf16[448,1024]{1,0:T(8,128)(2,1)S(1)}, bf16[448,1024]{1,0:T(8,128)(2,1)}, u32[]{:S(2)}, u32[]{:S(2)}) collective-permute-start(bf16[448,1024]{1,0:T(8,128)(2,1)S(1)} %collective-permute-done.3.refs_2_), channel_id=1, source_target_pairs={{0,8},{8,0},{1,9},{9,1},{2,10},{10,2},{3,11},{11,3},{4,12},{12,4},... | collective-permute-start | bytes 2752520 | tf_op jit(solution)/shard_map/ppermute | solution.py:100

commit v3 on v2

--- a/solution.py
+++ b/solution.py
@@ -44,6 +44,16 @@
     put(at_xh, slice(None), own_ref[...])
 
 
+def hidden_kernel(parts_ref, out_ref):
+    width = out_ref.shape[-1]
+    totals = parts_ref[0].astype(jnp.float32)
+    for i in range(1, parts_ref.shape[0]):
+        totals = totals + parts_ref[i].astype(jnp.float32)
+    hidden = (jax.nn.silu(totals[..., :width]) * totals[..., width:]).astype(out_ref.dtype)
+    for i in range(out_ref.shape[1]):
+        out_ref[:, i] = hidden
+
+
 def down_kernel(at_zb_ref, hidden_ref, *refs):
     *weight_refs, out_ref, joined_ref = refs
     width = weight_refs[0].shape[0]
@@ -65,7 +75,7 @@
         cost_estimate=pl.CostEstimate(
             flops=flops, bytes_accessed=2 * sum(a.size for a in args), transcendentals=0
         ),
-        compiler_params=pltpu.CompilerParams(vmem_limit_bytes=32 << 20),
+        compiler_params=pltpu.CompilerParams(vmem_limit_bytes=16 << 20),
     )(*args)
 
 
@@ -94,15 +104,13 @@
     )
     down_weight, partial = lax.optimization_barrier((down_weight, partial))
     down_far = lax.ppermute(down_weight, "zb", SWAP)
+    down_core = lax.ppermute(down_weight, "core", SWAP)
     parts = lax.all_to_all(partial.reshape(8, 2, 32, 4 * width), NARROW, 0, 0)
-    parts, down_weight, down_far = lax.optimization_barrier((parts, down_weight, down_far))
-    downs = [down_weight, lax.ppermute(down_weight, "core", SWAP)]
-    downs += [down_far, lax.ppermute(down_far, "core", SWAP)]
-
-    totals = total(parts)
-    hidden = (jax.nn.silu(totals[..., : 2 * width]) * totals[..., 2 * width :]).astype(jnp.bfloat16)
-    hidden = jnp.broadcast_to(hidden[:, None], (2, 8, 32, 2 * width)).reshape(16, 32, 2 * width)
-    hidden = lax.all_to_all(hidden, ("zb", *NARROW), 0, 0).reshape(2, n_rows, 2 * width)
+    hidden = call(hidden_kernel, [VMEM], (2, 8, 32, 2 * width), 16 * 64 * 4 * width, parts)
+    hidden, down_core, down_far = lax.optimization_barrier((hidden, down_core, down_far))
+    downs = [down_weight, down_core, down_far, lax.ppermute(down_far, "core", SWAP)]
+    hidden = lax.all_to_all(hidden.reshape(16, 32, 2 * width), ("zb", *NARROW), 0, 0)
+    hidden = hidden.reshape(2, n_rows, 2 * width)
     mixed = call(
         down_kernel,
         [SMEM] + [VMEM] * 5,

time: 140 us -> 137 us (0.979)
  other arithmetic: 2.6 us -> 0.72 us
    ppermute x1, waiting for transfers between devices: 13.6 us -> 0.25 us  [shards(): down_far = lax.ppermute(down_weight, 'zb', SWAP)]
    all_to_all x1, waiting for transfers between devices: 0.01 us -> 10.3 us  [shards(): parts = lax.all_to_all(partial.reshape(8, 2, 32, 4 * width), NARROW, 0, 0)]
    all_to_all x1, waiting for transfers between devices: 4.03 us -> 6.01 us  [shards(): lax.all_to_all(hidden.reshape(16, 32, 2 * width), ('zb', *NARROW), 0, 0)]
    reduce_sum x3 -> x2, other arithmetic: 2.52 us -> 0.72 us  [total(): return jnp.sum(parts.astype(jnp.float32), axis=0)]
    pallas_call x3 -> x4, Pallas kernels: 6.69 us -> 7.91 us  [call(): pl.pallas_call(kernel, out_shape=jax.ShapeDtypeStruct(out_shape, jnp.bflo...]
  transfers between devices with their start and end apart: 8 -> 8, of which waited for: 5 -> 5; matrix products, arithmetic and copies ran while one was open for 0% -> 0% of each run, Pallas kernels for 1% -> 2%
where the time goes in v3:
time: 137 us; the launch traced here: 136 us
  blocking collectives  75.1 us (55%)
  starting transfers between devices  26.7 us (19%)
  waiting for transfers between devices  23.2 us (17%)
  Pallas kernels  7.91 us (6%)
  local copies, waits for them, and re-layouts  2.36 us (2%)
    all_gather x1, blocking collectives, shards(): rows = lax.all_gather(tokens, ('zh', 'za', 'zb'), axis=0, tiled=True)  38.8 us
    all_to_all x1, blocking collectives, shards(): lax.all_to_all(mixed.astype(jnp.bfloat16).reshape(4, 16, depth), 'zh', 0, 0)  20.1 us
    all_to_all x1, blocking collectives, shards(): lax.all_to_all(mixed.reshape(4, 64, depth), ('za', 'xh'), 0, 0)  16.2 us
    all_to_all x1, waiting for transfers between devices, shards(): parts = lax.all_to_all(partial.reshape(8, 2, 32, 4 * width), NARROW, 0, 0)  10.3 us
    pallas_call x4, Pallas kernels, call(): pl.pallas_call(kernel, out_shape=jax.ShapeDtypeStruct(out_shape, jnp.bflo...  7.91 us
    all_to_all x1, waiting for transfers between devices, shards(): lax.all_to_all(hidden.reshape(16, 32, 2 * width), ('zb', *NARROW), 0, 0)  6.01 us
    all_to_all x1, starting transfers between devices, shards(): parts = lax.all_to_all(partial.reshape(8, 2, 32, 4 * width), NARROW, 0, 0)  5.97 us
    all_to_all x1, starting transfers between devices, shards(): lax.all_to_all(hidden.reshape(16, 32, 2 * width), ('zb', *NARROW), 0, 0)  5.72 us
  transfers between devices with their start and end apart: 8, of which 5 were waited for; matrix products, arithmetic and copies ran while one was open for 0% of the time, Pallas kernels for 2%

profile of v3, /device:TPU:8, one launch (start us, length us, event | category | flops | bytes accessed | tf_op | source)
XLA Modules:
  0.0 136.0 jit_solution(18156433507872623743)
XLA Ops:
  0.0 1.9 %collective-permute-start.1 = (bf16[448,1024]{1,0:T(8,128)(2,1)}, bf16[448,1024]{1,0:T(8,128)(2,1)S(1)}, u32[]{:S(2)}, u32[]{:S(2)}) collective-permute-start(bf16[448,1024]{1,0:T(8,128)(2,1)} %bitcast.9), channel_id=1, source_target_pairs={{0,8},{8,0},{1,9},{9,1},{2,10},{10,2},{3,11},{11,3},{4,12},{12,4},... | collective-permute-start | bytes 2752520 | tf_op jit(solution)/shard_map/ppermute | solution.py:88
  1.9 2.4 %collective-permute-start.2 = (bf16[448,1024]{1,0:T(8,128)(2,1)}, bf16[448,1024]{1,0:T(8,128)(2,1)S(1)}, u32[]{:S(2)}, u32[]{:S(2)}) collective-permute-start(bf16[448,1024]{1,0:T(8,128)(2,1)} %bitcast.12), channel_id=1, source_target_pairs={{0,8},{8,0},{1,9},{9,1},{2,10},{10,2},{3,11},{11,3},{4,12},{12,4},... | collective-permute-start | bytes 2752520 | tf_op jit(solution)/shard_map/ppermute | solution.py:88
  4.3 38.8 %all_gather.3.x_ref = bf16[256,1024]{1,0:T(8,128)(2,1)S(1)} all-gather(bf16[16,1024]{1,0:T(8,128)(2,1)} %param.4), channel_id=1, replica_groups=mesh['zh'=4,'za'=2,'zb'=2,'xh'=2,'core'=2,'xl'=2,'y'=4] {'zh','za','zb'}, dimensions={0}, use_global_device_ids=true | all-gather | bytes 557056 | tf_op jit(solution)/shard_map/all_gather | solution.py:90
  43.2 4.9 %collective-permute-start = (bf16[256,1024]{1,0:T(8,128)(2,1)S(1)}, bf16[256,1024]{1,0:T(8,128)(2,1)S(1)}, u32[]{:S(2)}, u32[]{:S(2)}) collective-permute-start(bf16[256,1024]{1,0:T(8,128)(2,1)S(1)} %all_gather.3.x_ref), channel_id=1, source_target_pairs={{0,16},{16,0},{1,17},{17,1},{2,18},{18,2},{3,19},{19,3},{4,20},{20... | collective-permute-start | bytes 1572872 | tf_op jit(solution)/shard_map/ppermute | solution.py:92
  48.1 0.0 collective-permute-done.1.refs_1_
  48.1 0.0 collective-permute-done.2.refs_3_
  48.1 0.0 copy-start
  48.1 1.2 copy-done
  49.3 0.0 copy-start.2
  49.3 1.2 copy-done.2
  50.5 0.0 copy-start.1
  50.5 0.0 copy-start.3
  50.5 1.3 shard_map.46.own_ref
  51.8 3.9 %collective-permute-done.x_ref = bf16[256,1024]{1,0:T(8,128)(2,1)S(1)} collective-permute-done((bf16[256,1024]{1,0:T(8,128)(2,1)S(1)}, bf16[256,1024]{1,0:T(8,128)(2,1)S(1)}, u32[]{:S(2)}, u32[]{:S(2)}) %collective-permute-start) | collective-permute-done | bytes 524320 | tf_op jit(solution)/shard_map/ppermute | solution.py:92
  55.7 0.0 copy-done.1
  55.7 0.0 copy-done.3
  55.7 2.7 %shard_map.47 = bf16[2,2,2,2,2,16,1792]{6,5,4,3,2,1,0:T(8,128)(2,1)} custom-call(s32[1]{0:T(128)} %bitcast.1.at_xh_ref, bf16[256,1024]{1,0:T(8,128)(2,1)S(1)} %collective-permute-done.x_ref, bf16[256,1792]{1,0:T(8,128)(2,1)S(1)} %shard_map.46.own_ref, bf16[448,1024]{1,0:T(8,128)(2,1)S(1)} %bitcast.11, bf16[448,1024]{1,0:T(8,128)(2,1)S(1)} %collective-permute-done.1.refs_1_, ...), custom_call_target="tpu_custom_call" | custom-call | flops 939524096 | bytes 5111810 | tf_op jit(solution)/shard_map/pallas_call | solution.py:69
  58.4 0.0 copy-start.4
  58.4 6.0 %all-to-all-start = ((bf16[8,2,32,1792]{3,2,1,0:T(8,128)(2,1)}), bf16[8,2,32,1792]{3,2,1,0:T(8,128)(2,1)S(1)}, u32[]{:S(2)}, u32[]{:S(2)}) async-start(bf16[8,2,32,1792]{3,2,1,0:T(8,128)(2,1)} %bitcast.4), calls=%async_computation | async-start | bytes 3670016 | tf_op jit(solution)/shard_map/all_to_all | solution.py:108
  64.4 0.0 copy-done.4
  64.4 1.9 %collective-permute-start.4 = (bf16[448,1024]{1,0:T(8,128)(2,1)S(1)}, bf16[448,1024]{1,0:T(8,128)(2,1)}, u32[]{:S(2)}, u32[]{:S(2)}) collective-permute-start(bf16[448,1024]{1,0:T(8,128)(2,1)S(1)} %copy-done.4), channel_id=1, source_target_pairs={{0,32},{32,0},{1,33},{33,1},{2,34},{34,2},{3,35},{35,3},{4,36},{36... | collective-permute-start | bytes 2752520 | tf_op jit(solution)/shard_map/ppermute | solution.py:106
  66.3 1.9 %collective-permute-start.3 = (bf16[448,1024]{1,0:T(8,128)(2,1)S(1)}, bf16[448,1024]{1,0:T(8,128)(2,1)}, u32[]{:S(2)}, u32[]{:S(2)}) collective-permute-start(bf16[448,1024]{1,0:T(8,128)(2,1)S(1)} %copy-done.4), channel_id=1, source_target_pairs={{0,8},{8,0},{1,9},{9,1},{2,10},{10,2},{3,11},{11,3},{4,12},{12,4},... | collective-permute-start | bytes 2752520 | tf_op jit(solution)/shard_map/ppermute | solution.py:107
  68.2 10.3 %all-to-all-done.parts_ref = bf16[8,2,32,1792]{3,2,1,0:T(8,128)(2,1)S(1)} async-done(((bf16[8,2,32,1792]{3,2,1,0:T(8,128)(2,1)}), bf16[8,2,32,1792]{3,2,1,0:T(8,128)(2,1)S(1)}, u32[]{:S(2)}, u32[]{:S(2)}) %all-to-all-start) | async-done | bytes 1835040 | tf_op jit(solution)/shard_map/all_to_all | solution.py:108
  78.6 1.2 shard_map.48
  79.8 0.3 collective-permute-done.4.refs_2_
  80.0 0.0 collective-permute-done.3.refs_1_
  80.0 5.7 %all-to-all-start.1 = ((bf16[16,32,896]{2,1,0:T(8,128)(2,1)}), bf16[16,32,896]{2,1,0:T(8,128)(2,1)S(1)}, u32[]{:S(2)}, u32[]{:S(2)}) async-start(bf16[16,32,896]{2,1,0:T(8,128)(2,1)} %bitcast.5), calls=%async_computation.1 | async-start | bytes 1835008 | tf_op jit(solution)/shard_map/all_to_all | solution.py:112
  85.8 1.9 %collective-permute-start.5 = (bf16[448,1024]{1,0:T(8,128)(2,1)}, bf16[448,1024]{1,0:T(8,128)(2,1)S(1)}, u32[]{:S(2)}, u32[]{:S(2)}) collective-permute-start(bf16[448,1024]{1,0:T(8,128)(2,1)} %collective-permute-done.4.refs_2_), channel_id=1, source_target_pairs={{0,8},{8,0},{1,9},{9,1},{2,10},{10,2},{3,11},{11,3},{4,12},{12,4},... | collective-permute-start | bytes 2752520 | tf_op jit(solution)/shard_map/ppermute | solution.py:111
  87.7 2.6 %collective-permute-done.5.refs_3_ = bf16[448,1024]{1,0:T(8,128)(2,1)S(1)} collective-permute-done((bf16[448,1024]{1,0:T(8,128)(2,1)}, bf16[448,1024]{1,0:T(8,128)(2,1)S(1)}, u32[]{:S(2)}, u32[]{:S(2)}) %collective-permute-start.5) | collective-permute-done | bytes 917536 | tf_op jit(solution)/shard_map/ppermute | solution.py:111
  90.3 6.0 %all-to-all-done.1 = bf16[16,32,896]{2,1,0:T(8,128)(2,1)S(1)} async-done(((bf16[16,32,896]{2,1,0:T(8,128)(2,1)}), bf16[16,32,896]{2,1,0:T(8,128)(2,1)S(1)}, u32[]{:S(2)}, u32[]{:S(2)}) %all-to-all-start.1) | async-done | bytes 917536 | tf_op jit(solution)/shard_map/all_to_all | solution.py:112
  96.3 2.7 %shard_map.49 = bf16[256,1024]{1,0:T(8,128)(2,1)S(1)} custom-call(s32[1]{0:T(128)} %bitcast.at_zb_ref, bf16[2,256,896]{2,1,0:T(8,128)(2,1)S(1)} %bitcast.15, bf16[448,1024]{1,0:T(8,128)(2,1)S(1)} %copy-done.4, bf16[448,1024]{1,0:T(8,128)(2,1)} %collective-permute-done.3.refs_1_, bf16[448,1024]{1,0:T(8,128)(2,1)} %collective-permute-done.4.refs_2_, ...), custom_call_target="tpu_custom_call" | custom-call | flops 939524096 | bytes 4587522 | tf_op jit(solution)/shard_map/pallas_call | solution.py:69
  99.0 16.2 %all_to_all.20 = bf16[4,64,1024]{2,1,0:T(8,128)(2,1)S(1)} all-to-all(bf16[4,64,1024]{2,1,0:T(8,128)(2,1)S(1)} %bitcast.16), channel_id=1, replica_groups=mesh['zh'=4,'za'=2,'zb'=2,'xh'=2,'core'=2,'xl'=2,'y'=4] {'za','xh'}, dimensions={0} | all-to-all | bytes 1048576 | tf_op jit(solution)/shard_map/all_to_all | solution.py:124
  115.2 0.1 reduce_sum.24
  115.3 20.1 %all_to_all.21 = bf16[4,16,1024]{2,1,0:T(8,128)(2,1)S(1)} all-to-all(bf16[4,16,1024]{2,1,0:T(8,128)(2,1)S(1)} %bitcast.17), channel_id=1, replica_groups=mesh['zh'=4,'za'=2,'zb'=2,'xh'=2,'core'=2,'xl'=2,'y'=4] {'zh'}, dimensions={0} | all-to-all | bytes 262144 | tf_op jit(solution)/shard_map/all_to_all | solution.py:125
  135.4 0.6 reduce_sum.25
Async XLA Ops:
  0.0 48.1 %collective-permute-start.1 = (bf16[448,1024]{1,0:T(8,128)(2,1)}, bf16[448,1024]{1,0:T(8,128)(2,1)S(1)}, u32[]{:S(2)}, u32[]{:S(2)}) collective-permute-start(bf16[448,1024]{1,0:T(8,128)(2,1)} %bitcast.9), channel_id=1, source_target_pairs={{0,8},{8,0},{1,9},{9,1},{2,10},{10,2},{3,11},{11,3},{4,12},{12,4},... | collective-permute-start | bytes 2752520 | tf_op jit(solution)/shard_map/ppermute | solution.py:88
  1.9 46.2 %collective-permute-start.2 = (bf16[448,1024]{1,0:T(8,128)(2,1)}, bf16[448,1024]{1,0:T(8,128)(2,1)S(1)}, u32[]{:S(2)}, u32[]{:S(2)}) collective-permute-start(bf16[448,1024]{1,0:T(8,128)(2,1)} %bitcast.12), channel_id=1, source_target_pairs={{0,8},{8,0},{1,9},{9,1},{2,10},{10,2},{3,11},{11,3},{4,12},{12,4},... | collective-permute-start | bytes 2752520 | tf_op jit(solution)/shard_map/ppermute | solution.py:88
  43.2 12.6 %collective-permute-start = (bf16[256,1024]{1,0:T(8,128)(2,1)S(1)}, bf16[256,1024]{1,0:T(8,128)(2,1)S(1)}, u32[]{:S(2)}, u32[]{:S(2)}) collective-permute-start(bf16[256,1024]{1,0:T(8,128)(2,1)S(1)} %all_gather.3.x_ref), channel_id=1, source_target_pairs={{0,16},{16,0},{1,17},{17,1},{2,18},{18,2},{3,19},{19,3},{4,20},{20... | collective-permute-start | bytes 1572872 | tf_op jit(solution)/shard_map/ppermute | solution.py:92
  48.1 1.2 copy-start
  49.3 1.2 copy-start.2
  50.5 5.3 %copy-start.1 = (bf16[1024,448]{0,1:T(8,128)(2,1)S(1)}, bf16[1024,448]{0,1:T(8,128)(2,1)}, u32[]{:S(2)}) copy-start(bf16[1024,448]{0,1:T(8,128)(2,1)} %param.5) | copy-start | bytes 2752516
  50.5 5.3 %copy-start.3 = (bf16[1024,448]{0,1:T(8,128)(2,1)S(1)}, bf16[1024,448]{0,1:T(8,128)(2,1)}, u32[]{:S(2)}) copy-start(bf16[1024,448]{0,1:T(8,128)(2,1)} %param.6) | copy-start | bytes 2752516
  58.4 6.0 %copy-start.4 = (bf16[448,1024]{1,0:T(8,128)(2,1)S(1)}, bf16[448,1024]{1,0:T(8,128)(2,1)}, u32[]{:S(2)}) copy-start(bf16[448,1024]{1,0:T(8,128)(2,1)} %refs_0_) | copy-start | bytes 2752516
  58.4 20.2 %all-to-all-start = ((bf16[8,2,32,1792]{3,2,1,0:T(8,128)(2,1)}), bf16[8,2,32,1792]{3,2,1,0:T(8,128)(2,1)S(1)}, u32[]{:S(2)}, u32[]{:S(2)}) async-start(bf16[8,2,32,1792]{3,2,1,0:T(8,128)(2,1)} %bitcast.4), calls=%async_computation | async-start | bytes 3670016 | tf_op jit(solution)/shard_map/all_to_all | solution.py:108
  64.4 15.6 %collective-permute-start.4 = (bf16[448,1024]{1,0:T(8,128)(2,1)S(1)}, bf16[448,1024]{1,0:T(8,128)(2,1)}, u32[]{:S(2)}, u32[]{:S(2)}) collective-permute-start(bf16[448,1024]{1,0:T(8,128)(2,1)S(1)} %copy-done.4), channel_id=1, source_target_pairs={{0,32},{32,0},{1,33},{33,1},{2,34},{34,2},{3,35},{35,3},{4,36},{36... | collective-permute-start | bytes 2752520 | tf_op jit(solution)/shard_map/ppermute | solution.py:106
  66.3 13.7 %collective-permute-start.3 = (bf16[448,1024]{1,0:T(8,128)(2,1)S(1)}, bf16[448,1024]{1,0:T(8,128)(2,1)}, u32[]{:S(2)}, u32[]{:S(2)}) collective-permute-start(bf16[448,1024]{1,0:T(8,128)(2,1)S(1)} %copy-done.4), channel_id=1, source_target_pairs={{0,8},{8,0},{1,9},{9,1},{2,10},{10,2},{3,11},{11,3},{4,12},{12,4},... | collective-permute-start | bytes 2752520 | tf_op jit(solution)/shard_map/ppermute | solution.py:107
  80.0 16.3 %all-to-all-start.1 = ((bf16[16,32,896]{2,1,0:T(8,128)(2,1)}), bf16[16,32,896]{2,1,0:T(8,128)(2,1)S(1)}, u32[]{:S(2)}, u32[]{:S(2)}) async-start(bf16[16,32,896]{2,1,0:T(8,128)(2,1)} %bitcast.5), calls=%async_computation.1 | async-start | bytes 1835008 | tf_op jit(solution)/shard_map/all_to_all | solution.py:112
  85.8 4.6 %collective-permute-start.5 = (bf16[448,1024]{1,0:T(8,128)(2,1)}, bf16[448,1024]{1,0:T(8,128)(2,1)S(1)}, u32[]{:S(2)}, u32[]{:S(2)}) collective-permute-start(bf16[448,1024]{1,0:T(8,128)(2,1)} %collective-permute-done.4.refs_2_), channel_id=1, source_target_pairs={{0,8},{8,0},{1,9},{9,1},{2,10},{10,2},{3,11},{11,3},{4,12},{12,4},... | collective-permute-start | bytes 2752520 | tf_op jit(solution)/shard_map/ppermute | solution.py:111

commit v4 on v3

v4 whole, which is shorter than its diff:
```python
import jax
import jax.numpy as jnp
from jax import lax
from jax.experimental import pallas as pl
from jax.experimental.pallas import tpu as pltpu
from jax.sharding import Mesh, PartitionSpec as P

AXES = ("zh", "za", "zb", "xh", "core", "xl", "y")
NARROW = ("xl", "y")
SWAP = [(0, 1), (1, 0)]
VMEM = pl.BlockSpec(memory_space=pltpu.VMEM)
SMEM = pl.BlockSpec(memory_space=pltpu.SMEM)
HBM = pl.BlockSpec(memory_space=pltpu.HBM)


def total(parts):
    return jnp.sum(parts.astype(jnp.float32), axis=0)


def matmul(a, b, b_dim):
    return lax.dot_general(a, b, (((1,), (b_dim,)), ((), ())), preferred_element_type=jnp.float32)


def project_kernel(slot_ref, x_ref, *refs):
    out_ref, block_ref, sems = refs[-3:]
    weight_refs = refs[:4]
    width = weight_refs[0].shape[0]
    copies = []
    for i, w_ref in enumerate(weight_refs):
        product = matmul(x_ref[...], w_ref[...], 1).astype(out_ref.dtype)
        columns = slice(i * width, (i + 1) * width)
        for at in range(16):
            high, low, za, zb = at // 8, at // 4 % 2, at // 2 % 2, at % 2
            block_ref[za, high, zb, low, :, columns] = product[at * 16 : (at + 1) * 16]
        if i % 2:
            half = pl.ds((i - 1) * width, 2 * width)
            copies.append(
                pltpu.make_async_copy(
                    block_ref.at[..., half],
                    out_ref.at[slot_ref[0], :, :, :, :, :, half],
                    sems.at[i // 2],
                )
            )
            copies[-1].start()
    for copy in copies:
        copy.wait()


def hidden_kernel(parts_ref, out_ref):
    width = out_ref.shape[-1]
    totals = parts_ref[0].astype(jnp.float32)
    for i in range(1, parts_ref.shape[0]):
        totals = totals + parts_ref[i].astype(jnp.float32)
    hidden = (jax.nn.silu(totals[..., :width]) * totals[..., width:]).astype(out_ref.dtype)
    for i in range(out_ref.shape[0]):
        out_ref[i] = hidden


def down_kernel(at_zb_ref, hidden_ref, *refs):
    *weight_refs, out_ref = refs
    width = weight_refs[0].shape[0]
    at_zb = at_zb_ref[0]
    mixed = 0.0
    for i, w_ref in enumerate(weight_refs):
        units = hidden_ref[:, at_zb if i < 2 else 1 - at_zb, :, i % 2 * width : (i % 2 + 1) * width]
        mixed = mixed + matmul(units.reshape(out_ref.shape[0], width), w_ref[...], 0)
    out_ref[...] = mixed.astype(out_ref.dtype)


def call(kernel, specs, out_shape, flops, *args, out_spec=VMEM, scratch=(), aliases={}):
    return pl.pallas_call(
        kernel,
        out_shape=jax.ShapeDtypeStruct(out_shape, jnp.bfloat16),
        in_specs=specs,
        out_specs=out_spec,
        input_output_aliases=aliases,
        scratch_shapes=scratch,
        cost_estimate=pl.CostEstimate(
            flops=flops, bytes_accessed=2 * sum(a.size for a in args), transcendentals=0
        ),
        compiler_params=pltpu.CompilerParams(vmem_limit_bytes=16 << 20),
    )(*args)


def shards(tokens, gate_weight, up_weight, down_weight):
    depth = tokens.shape[1]
    at_xh = lax.axis_index("xh").reshape(1)
    at_zb = lax.axis_index("zb").reshape(1)
    gate, up = gate_weight.T, up_weight.T
    width = gate.shape[0]
    weights = [gate, lax.ppermute(gate, "core", SWAP), up, lax.ppermute(up, "core", SWAP)]

    rows = lax.all_gather(tokens, ("zh", "za", "zb"), axis=0, tiled=True)
    n_rows = rows.shape[0]
    other_rows = lax.ppermute(rows, "xh", SWAP)
    flops = 8 * n_rows * depth * width

    def project(slot, x, *started):
        return call(
            project_kernel,
            [SMEM] + [VMEM] * 5 + [HBM] * len(started),
            (2, 2, 2, 2, 2, 16, 4 * width),
            flops,
            slot,
            x,
            *weights,
            *started,
            out_spec=HBM,
            scratch=[
                pltpu.VMEM((2, 2, 2, 2, 16, 4 * width), jnp.bfloat16),
                pltpu.SemaphoreType.DMA((2,)),
            ],
            aliases={6: 0} if started else {},
        )

    partial = project(1 - at_xh, other_rows, project(at_xh, rows))
    down_weight, partial = lax.optimization_barrier((down_weight, partial))
    down_far = lax.ppermute(down_weight, "zb", SWAP)
    down_core = lax.ppermute(down_weight, "core", SWAP)
    parts = lax.all_to_all(partial.reshape(8, 2, 32, 4 * width), NARROW, 0, 0)
    hidden = call(hidden_kernel, [VMEM], (8, 2, 32, 2 * width), 16 * 64 * 4 * width, parts)
    hidden, down_core, down_far = lax.optimization_barrier((hidden, down_core, down_far))
    downs = [down_weight, down_core, down_far, lax.ppermute(down_far, "core", SWAP)]
    hidden = lax.all_to_all(hidden.reshape(16, 32, 2 * width), (*NARROW, "zb"), 0, 0)
    hidden = hidden.reshape(8, 2, 32, 2 * width)
    mixed = call(
        down_kernel,
        [SMEM] + [VMEM] * 5,
        (n_rows, depth),
        8 * n_rows * depth * width,
        at_zb,
        hidden,
        *downs,
    )
    mixed = total(lax.all_to_all(mixed.reshape(4, 64, depth), ("xh", "za"), 0, 0))
    mixed = lax.all_to_all(mixed.astype(jnp.bfloat16).reshape(4, 16, depth), "zh", 0, 0)
    return total(mixed).astype(jnp.bfloat16)


def solution(mesh):
    fine = Mesh(mesh.devices.reshape(4, 2, 2, 2, 2, 2, 4), AXES)
    loop = ("zh", "za", "zb", "xh", "core")
    return jax.shard_map(
        shards,
        mesh=fine,
        in_specs=(P(loop, NARROW), P(NARROW, loop), P(NARROW, loop), P(loop, NARROW)),
        out_specs=P(loop, NARROW),
        check_vma=False,
    )
```

time: 137 us -> 135 us (0.985)
  the two profiles are of different devices: /device:TPU:8 before, /device:TPU:2 now
where the time goes in v4:
time: 135 us
  blocking collectives  74.5 us (55%)
  starting transfers between devices  25.5 us (19%)
  waiting for transfers between devices  23 us (17%)
  Pallas kernels  8.31 us (6%)
  local copies, waits for them, and re-layouts  2.37 us (2%)
    all_gather x1, blocking collectives, shards(): rows = lax.all_gather(tokens, ('zh', 'za', 'zb'), axis=0, tiled=True)  38.8 us
    all_to_all x1, blocking collectives, shards(): lax.all_to_all(mixed.astype(jnp.bfloat16).reshape(4, 16, depth), 'zh', 0, 0)  20.2 us
    all_to_all x1, blocking collectives, shards(): lax.all_to_all(mixed.reshape(4, 64, depth), ('xh', 'za'), 0, 0)  15.5 us
    all_to_all x1, waiting for transfers between devices, shards(): parts = lax.all_to_all(partial.reshape(8, 2, 32, 4 * width), NARROW, 0, 0)  10.9 us
    pallas_call x4, Pallas kernels, call(): pl.pallas_call(kernel, out_shape=jax.ShapeDtypeStruct(out_shape, jnp.bflo...  8.31 us
    all_to_all x1, starting transfers between devices, shards(): parts = lax.all_to_all(partial.reshape(8, 2, 32, 4 * width), NARROW, 0, 0)  6.07 us
    all_to_all x1, waiting for transfers between devices, shards(): lax.all_to_all(hidden.reshape(16, 32, 2 * width), (*NARROW, 'zb'), 0, 0)  5.42 us
    all_to_all x1, starting transfers between devices, shards(): lax.all_to_all(hidden.reshape(16, 32, 2 * width), (*NARROW, 'zb'), 0, 0)  5.37 us
  transfers between devices with their start and end apart: 8, of which 4 were waited for; matrix products, arithmetic and copies ran while one was open for 0% of the time, Pallas kernels for 3%

profile of v4, /device:TPU:2, one launch (start us, length us, event | category | flops | bytes accessed | tf_op | source)
XLA Modules:
  0.0 134.5 jit_solution(14070711742127217139)
XLA Ops:
  0.0 1.9 %collective-permute-start.1 = (bf16[448,1024]{1,0:T(8,128)(2,1)}, bf16[448,1024]{1,0:T(8,128)(2,1)S(1)}, u32[]{:S(2)}, u32[]{:S(2)}) collective-permute-start(bf16[448,1024]{1,0:T(8,128)(2,1)} %bitcast.9), channel_id=1, source_target_pairs={{0,8},{8,0},{1,9},{9,1},{2,10},{10,2},{3,11},{11,3},{4,12},{12,4},... | collective-permute-start | bytes 2752520 | tf_op jit(solution)/shard_map/ppermute | solution.py:91
  1.9 2.4 %collective-permute-start.2 = (bf16[448,1024]{1,0:T(8,128)(2,1)}, bf16[448,1024]{1,0:T(8,128)(2,1)S(1)}, u32[]{:S(2)}, u32[]{:S(2)}) collective-permute-start(bf16[448,1024]{1,0:T(8,128)(2,1)} %bitcast.12), channel_id=1, source_target_pairs={{0,8},{8,0},{1,9},{9,1},{2,10},{10,2},{3,11},{11,3},{4,12},{12,4},... | collective-permute-start | bytes 2752520 | tf_op jit(solution)/shard_map/ppermute | solution.py:91
  4.3 38.8 %all_gather.3.x_ref = bf16[256,1024]{1,0:T(8,128)(2,1)S(1)} all-gather(bf16[16,1024]{1,0:T(8,128)(2,1)} %param.4), channel_id=1, replica_groups=mesh['zh'=4,'za'=2,'zb'=2,'xh'=2,'core'=2,'xl'=2,'y'=4] {'zh','za','zb'}, dimensions={0}, use_global_device_ids=true | all-gather | bytes 557056 | tf_op jit(solution)/shard_map/all_gather | solution.py:93
  43.2 4.0 %collective-permute-start = (bf16[256,1024]{1,0:T(8,128)(2,1)S(1)}, bf16[256,1024]{1,0:T(8,128)(2,1)S(1)}, u32[]{:S(2)}, u32[]{:S(2)}) collective-permute-start(bf16[256,1024]{1,0:T(8,128)(2,1)S(1)} %all_gather.3.x_ref), channel_id=1, source_target_pairs={{0,16},{16,0},{1,17},{17,1},{2,18},{18,2},{3,19},{19,3},{4,20},{20... | collective-permute-start | bytes 1572872 | tf_op jit(solution)/shard_map/ppermute | solution.py:95
  47.2 0.0 collective-permute-done.1.refs_1_
  47.2 0.0 collective-permute-done.2.refs_3_
  47.2 0.0 copy-start
  47.2 1.2 copy-done
  48.4 0.0 copy-start.2
  48.4 1.2 copy-done.2
  49.6 0.0 copy-start.1
  49.6 0.0 copy-start.3
  49.6 2.2 %shard_map.46.refs_4_ = bf16[2,2,2,2,2,16,1792]{6,5,4,3,2,1,0:T(8,128)(2,1)} custom-call(s32[1]{0:T(128)} %bitcast.1.slot_ref, bf16[256,1024]{1,0:T(8,128)(2,1)S(1)} %all_gather.3.x_ref, bf16[448,1024]{1,0:T(8,128)(2,1)S(1)} %bitcast.10, bf16[448,1024]{1,0:T(8,128)(2,1)S(1)} %collective-permute-done.1.refs_1_, bf16[448,1024]{1,0:T(8,128)(2,1)S(1)} %bitcast.13, ...), custom_call_target="tpu_custom_call" | custom-call | flops 939524096 | bytes 4194306 | tf_op jit(solution)/shard_map/pallas_call | solution.py:71
  51.8 4.0 %collective-permute-done.x_ref = bf16[256,1024]{1,0:T(8,128)(2,1)S(1)} collective-permute-done((bf16[256,1024]{1,0:T(8,128)(2,1)S(1)}, bf16[256,1024]{1,0:T(8,128)(2,1)S(1)}, u32[]{:S(2)}, u32[]{:S(2)}) %collective-permute-start) | collective-permute-done | bytes 524320 | tf_op jit(solution)/shard_map/ppermute | solution.py:95
  55.7 0.0 copy-done.1
  55.7 0.0 copy-done.3
  55.7 2.2 %shard_map.47 = bf16[2,2,2,2,2,16,1792]{6,5,4,3,2,1,0:T(8,128)(2,1)} custom-call(s32[1]{0:T(128)S(6)} %sub.3.slot_ref, bf16[256,1024]{1,0:T(8,128)(2,1)S(1)} %collective-permute-done.x_ref, bf16[448,1024]{1,0:T(8,128)(2,1)S(1)} %bitcast.11, bf16[448,1024]{1,0:T(8,128)(2,1)S(1)} %collective-permute-done.1.refs_1_, ...), custom_call_target="tpu_custom_call", output_to_operand_aliasing={{}: (6, {})} | custom-call | flops 939524096 | bytes 6029314 | tf_op jit(solution)/shard_map/pallas_call | solution.py:71
  57.9 0.0 copy-start.4
  57.9 6.1 %all-to-all-start = ((bf16[8,2,32,1792]{3,2,1,0:T(8,128)(2,1)}), bf16[8,2,32,1792]{3,2,1,0:T(8,128)(2,1)S(1)}, u32[]{:S(2)}, u32[]{:S(2)}) async-start(bf16[8,2,32,1792]{3,2,1,0:T(8,128)(2,1)} %bitcast.4), calls=%async_computation | async-start | bytes 3670016 | tf_op jit(solution)/shard_map/all_to_all | solution.py:120
  64.0 0.0 copy-done.4
  64.0 1.9 %collective-permute-start.4 = (bf16[448,1024]{1,0:T(8,128)(2,1)S(1)}, bf16[448,1024]{1,0:T(8,128)(2,1)}, u32[]{:S(2)}, u32[]{:S(2)}) collective-permute-start(bf16[448,1024]{1,0:T(8,128)(2,1)S(1)} %copy-done.4), channel_id=1, source_target_pairs={{0,32},{32,0},{1,33},{33,1},{2,34},{34,2},{3,35},{35,3},{4,36},{36... | collective-permute-start | bytes 2752520 | tf_op jit(solution)/shard_map/ppermute | solution.py:118
  65.9 1.9 %collective-permute-start.3 = (bf16[448,1024]{1,0:T(8,128)(2,1)S(1)}, bf16[448,1024]{1,0:T(8,128)(2,1)}, u32[]{:S(2)}, u32[]{:S(2)}) collective-permute-start(bf16[448,1024]{1,0:T(8,128)(2,1)S(1)} %copy-done.4), channel_id=1, source_target_pairs={{0,8},{8,0},{1,9},{9,1},{2,10},{10,2},{3,11},{11,3},{4,12},{12,4},... | collective-permute-start | bytes 2752520 | tf_op jit(solution)/shard_map/ppermute | solution.py:119
  67.9 10.9 %all-to-all-done.parts_ref = bf16[8,2,32,1792]{3,2,1,0:T(8,128)(2,1)S(1)} async-done(((bf16[8,2,32,1792]{3,2,1,0:T(8,128)(2,1)}), bf16[8,2,32,1792]{3,2,1,0:T(8,128)(2,1)S(1)}, u32[]{:S(2)}, u32[]{:S(2)}) %all-to-all-start) | async-done | bytes 1835040 | tf_op jit(solution)/shard_map/all_to_all | solution.py:120
  78.8 1.2 shard_map.48
  80.0 0.0 collective-permute-done.4.refs_2_
  80.0 0.0 collective-permute-done.3.refs_1_
  80.0 5.4 %all-to-all-start.1 = ((bf16[16,32,896]{2,1,0:T(8,128)(2,1)}), bf16[16,32,896]{2,1,0:T(8,128)(2,1)S(1)}, u32[]{:S(2)}, u32[]{:S(2)}) async-start(bf16[16,32,896]{2,1,0:T(8,128)(2,1)} %bitcast.5), calls=%async_computation.1 | async-start | bytes 1835008 | tf_op jit(solution)/shard_map/all_to_all | solution.py:124
  85.4 1.9 %collective-permute-start.5 = (bf16[448,1024]{1,0:T(8,128)(2,1)}, bf16[448,1024]{1,0:T(8,128)(2,1)S(1)}, u32[]{:S(2)}, u32[]{:S(2)}) collective-permute-start(bf16[448,1024]{1,0:T(8,128)(2,1)} %collective-permute-done.4.refs_2_), channel_id=1, source_target_pairs={{0,8},{8,0},{1,9},{9,1},{2,10},{10,2},{3,11},{11,3},{4,12},{12,4},... | collective-permute-start | bytes 2752520 | tf_op jit(solution)/shard_map/ppermute | solution.py:123
  87.3 2.6 %collective-permute-done.5.refs_3_ = bf16[448,1024]{1,0:T(8,128)(2,1)S(1)} collective-permute-done((bf16[448,1024]{1,0:T(8,128)(2,1)}, bf16[448,1024]{1,0:T(8,128)(2,1)S(1)}, u32[]{:S(2)}, u32[]{:S(2)}) %collective-permute-start.5) | collective-permute-done | bytes 917536 | tf_op jit(solution)/shard_map/ppermute | solution.py:123
  89.9 5.4 %all-to-all-done.1 = bf16[16,32,896]{2,1,0:T(8,128)(2,1)S(1)} async-done(((bf16[16,32,896]{2,1,0:T(8,128)(2,1)}), bf16[16,32,896]{2,1,0:T(8,128)(2,1)S(1)}, u32[]{:S(2)}, u32[]{:S(2)}) %all-to-all-start.1) | async-done | bytes 917536 | tf_op jit(solution)/shard_map/all_to_all | solution.py:124
  95.4 2.7 %shard_map.49 = bf16[256,1024]{1,0:T(8,128)(2,1)S(1)} custom-call(s32[1]{0:T(128)} %bitcast.at_zb_ref, bf16[8,2,32,896]{3,2,1,0:T(8,128)(2,1)S(1)} %bitcast.15, bf16[448,1024]{1,0:T(8,128)(2,1)S(1)} %copy-done.4, bf16[448,1024]{1,0:T(8,128)(2,1)} %collective-permute-done.3.refs_1_, bf16[448,1024]{1,0:T(8,128)(2,1)} %collective-permute-done.4.refs_2_, ...), custom_call_target="tpu_custom_call" | custom-call | flops 939524096 | bytes 4587522 | tf_op jit(solution)/shard_map/pallas_call | solution.py:71
  98.1 15.5 %all_to_all.20 = bf16[4,64,1024]{2,1,0:T(8,128)(2,1)S(1)} all-to-all(bf16[4,64,1024]{2,1,0:T(8,128)(2,1)S(1)} %bitcast.16), channel_id=1, replica_groups=mesh['zh'=4,'za'=2,'zb'=2,'xh'=2,'core'=2,'xl'=2,'y'=4] {'xh','za'}, dimensions={0} | all-to-all | bytes 1048576 | tf_op jit(solution)/shard_map/all_to_all | solution.py:135
  113.6 0.1 reduce_sum.24
  113.7 20.2 %all_to_all.21 = bf16[4,16,1024]{2,1,0:T(8,128)(2,1)S(1)} all-to-all(bf16[4,16,1024]{2,1,0:T(8,128)(2,1)S(1)} %bitcast.17), channel_id=1, replica_groups=mesh['zh'=4,'za'=2,'zb'=2,'xh'=2,'core'=2,'xl'=2,'y'=4] {'zh'}, dimensions={0} | all-to-all | bytes 262144 | tf_op jit(solution)/shard_map/all_to_all | solution.py:136
  133.9 0.6 reduce_sum.25
Async XLA Ops:
  0.0 47.2 %collective-permute-start.1 = (bf16[448,1024]{1,0:T(8,128)(2,1)}, bf16[448,1024]{1,0:T(8,128)(2,1)S(1)}, u32[]{:S(2)}, u32[]{:S(2)}) collective-permute-start(bf16[448,1024]{1,0:T(8,128)(2,1)} %bitcast.9), channel_id=1, source_target_pairs={{0,8},{8,0},{1,9},{9,1},{2,10},{10,2},{3,11},{11,3},{4,12},{12,4},... | collective-permute-start | bytes 2752520 | tf_op jit(solution)/shard_map/ppermute | solution.py:91
  1.9 45.3 %collective-permute-start.2 = (bf16[448,1024]{1,0:T(8,128)(2,1)}, bf16[448,1024]{1,0:T(8,128)(2,1)S(1)}, u32[]{:S(2)}, u32[]{:S(2)}) collective-permute-start(bf16[448,1024]{1,0:T(8,128)(2,1)} %bitcast.12), channel_id=1, source_target_pairs={{0,8},{8,0},{1,9},{9,1},{2,10},{10,2},{3,11},{11,3},{4,12},{12,4},... | collective-permute-start | bytes 2752520 | tf_op jit(solution)/shard_map/ppermute | solution.py:91
  43.2 12.6 %collective-permute-start = (bf16[256,1024]{1,0:T(8,128)(2,1)S(1)}, bf16[256,1024]{1,0:T(8,128)(2,1)S(1)}, u32[]{:S(2)}, u32[]{:S(2)}) collective-permute-start(bf16[256,1024]{1,0:T(8,128)(2,1)S(1)} %all_gather.3.x_ref), channel_id=1, source_target_pairs={{0,16},{16,0},{1,17},{17,1},{2,18},{18,2},{3,19},{19,3},{4,20},{20... | collective-permute-start | bytes 1572872 | tf_op jit(solution)/shard_map/ppermute | solution.py:95
  47.2 1.2 copy-start
  48.4 1.2 copy-start.2
  49.6 6.2 %copy-start.1 = (bf16[1024,448]{0,1:T(8,128)(2,1)S(1)}, bf16[1024,448]{0,1:T(8,128)(2,1)}, u32[]{:S(2)}) copy-start(bf16[1024,448]{0,1:T(8,128)(2,1)} %param.5) | copy-start | bytes 2752516
  49.6 6.2 %copy-start.3 = (bf16[1024,448]{0,1:T(8,128)(2,1)S(1)}, bf16[1024,448]{0,1:T(8,128)(2,1)}, u32[]{:S(2)}) copy-start(bf16[1024,448]{0,1:T(8,128)(2,1)} %param.6) | copy-start | bytes 2752516
  57.9 6.1 %copy-start.4 = (bf16[448,1024]{1,0:T(8,128)(2,1)S(1)}, bf16[448,1024]{1,0:T(8,128)(2,1)}, u32[]{:S(2)}) copy-start(bf16[448,1024]{1,0:T(8,128)(2,1)} %refs_0_) | copy-start | bytes 2752516
  57.9 20.9 %all-to-all-start = ((bf16[8,2,32,1792]{3,2,1,0:T(8,128)(2,1)}), bf16[8,2,32,1792]{3,2,1,0:T(8,128)(2,1)S(1)}, u32[]{:S(2)}, u32[]{:S(2)}) async-start(bf16[8,2,32,1792]{3,2,1,0:T(8,128)(2,1)} %bitcast.4), calls=%async_computation | async-start | bytes 3670016 | tf_op jit(solution)/shard_map/all_to_all | solution.py:120
  64.0 16.0 %collective-permute-start.4 = (bf16[448,1024]{1,0:T(8,128)(2,1)S(1)}, bf16[448,1024]{1,0:T(8,128)(2,1)}, u32[]{:S(2)}, u32[]{:S(2)}) collective-permute-start(bf16[448,1024]{1,0:T(8,128)(2,1)S(1)} %copy-done.4), channel_id=1, source_target_pairs={{0,32},{32,0},{1,33},{33,1},{2,34},{34,2},{3,35},{35,3},{4,36},{36... | collective-permute-start | bytes 2752520 | tf_op jit(solution)/shard_map/ppermute | solution.py:118
  65.9 14.1 %collective-permute-start.3 = (bf16[448,1024]{1,0:T(8,128)(2,1)S(1)}, bf16[448,1024]{1,0:T(8,128)(2,1)}, u32[]{:S(2)}, u32[]{:S(2)}) collective-permute-start(bf16[448,1024]{1,0:T(8,128)(2,1)S(1)} %copy-done.4), channel_id=1, source_target_pairs={{0,8},{8,0},{1,9},{9,1},{2,10},{10,2},{3,11},{11,3},{4,12},{12,4},... | collective-permute-start | bytes 2752520 | tf_op jit(solution)/shard_map/ppermute | solution.py:119
  80.0 15.4 %all-to-all-start.1 = ((bf16[16,32,896]{2,1,0:T(8,128)(2,1)}), bf16[16,32,896]{2,1,0:T(8,128)(2,1)S(1)}, u32[]{:S(2)}, u32[]{:S(2)}) async-start(bf16[16,32,896]{2,1,0:T(8,128)(2,1)} %bitcast.5), calls=%async_computation.1 | async-start | bytes 1835008 | tf_op jit(solution)/shard_map/all_to_all | solution.py:124
  85.4 4.6 %collective-permute-start.5 = (bf16[448,1024]{1,0:T(8,128)(2,1)}, bf16[448,1024]{1,0:T(8,128)(2,1)S(1)}, u32[]{:S(2)}, u32[]{:S(2)}) collective-permute-start(bf16[448,1024]{1,0:T(8,128)(2,1)} %collective-permute-done.4.refs_2_), channel_id=1, source_target_pairs={{0,8},{8,0},{1,9},{9,1},{2,10},{10,2},{3,11},{11,3},{4,12},{12,4},... | collective-permute-start | bytes 2752520 | tf_op jit(solution)/shard_map/ppermute | solution.py:123

commit v5 on v4

--- a/solution.py
+++ b/solution.py
@@ -8,6 +8,27 @@
 AXES = ("zh", "za", "zb", "xh", "core", "xl", "y")
 NARROW = ("xl", "y")
 SWAP = [(0, 1), (1, 0)]
+LOOP = ("zh", "za", "zb", "xh", "core")
+GROUPS = ((0, 3, 6, 1), (7, 4, 5, 2))
+
+
+def loop_at(pair, zb, xh, core):
+    return pair * 8 + zb * 4 + xh * 2 + core
+
+
+NEAR = [
+    [loop_at(group[at], zb, xh, core) for xh in range(2) for group in GROUPS]
+    for at in range(4)
+    for zb in range(2)
+    for core in range(2)
+]
+FAR = [
+    [loop_at(pair, zb, xh, core) for pair in group]
+    for group in GROUPS
+    for zb in range(2)
+    for xh in range(2)
+    for core in range(2)
+]
 VMEM = pl.BlockSpec(memory_space=pltpu.VMEM)
 SMEM = pl.BlockSpec(memory_space=pltpu.SMEM)
 HBM = pl.BlockSpec(memory_space=pltpu.HBM)
@@ -30,8 +51,9 @@
         product = matmul(x_ref[...], w_ref[...], 1).astype(out_ref.dtype)
         columns = slice(i * width, (i + 1) * width)
         for at in range(16):
-            high, low, za, zb = at // 8, at // 4 % 2, at // 2 % 2, at % 2
-            block_ref[za, high, zb, low, :, columns] = product[at * 16 : (at + 1) * 16]
+            za = int(at // 2 in GROUPS[1])
+            place, zb = GROUPS[za].index(at // 2), at % 2
+            block_ref[za, place // 2, zb, place % 2, :, columns] = product[at * 16 : (at + 1) * 16]
         if i % 2:
             half = pl.ds((i - 1) * width, 2 * width)
             copies.append(
@@ -57,13 +79,22 @@
 
 
 def down_kernel(at_zb_ref, hidden_ref, *refs):
-    *weight_refs, out_ref = refs
+    *weight_refs, out_ref, fetched_ref, sems = refs
     width = weight_refs[0].shape[0]
     at_zb = at_zb_ref[0]
+    copies = [
+        pltpu.make_async_copy(weight_refs[1 + i], fetched_ref.at[i], sems.at[i]) for i in range(2)
+    ]
+    for copy in copies:
+        copy.start()
     mixed = 0.0
-    for i, w_ref in enumerate(weight_refs):
-        units = hidden_ref[:, at_zb if i < 2 else 1 - at_zb, :, i % 2 * width : (i % 2 + 1) * width]
-        mixed = mixed + matmul(units.reshape(out_ref.shape[0], width), w_ref[...], 0)
+    for i in (0, 3, 1, 2):
+        side = at_zb if i < 2 else 1 - at_zb
+        units = hidden_ref[:, side, :, i % 2 * width : (i % 2 + 1) * width]
+        if i in (1, 2):
+            copies[i - 1].wait()
+        weight = fetched_ref[i - 1] if i in (1, 2) else weight_refs[i][...]
+        mixed = mixed + matmul(units.reshape(out_ref.shape[0], width), weight, 0)
     out_ref[...] = mixed.astype(out_ref.dtype)
 
 
@@ -125,15 +156,19 @@
     hidden = hidden.reshape(8, 2, 32, 2 * width)
     mixed = call(
         down_kernel,
-        [SMEM] + [VMEM] * 5,
+        [SMEM, VMEM, VMEM, HBM, HBM, VMEM],
         (n_rows, depth),
         8 * n_rows * depth * width,
         at_zb,
         hidden,
         *downs,
+        scratch=[
+            pltpu.VMEM((2, width, depth), jnp.bfloat16),
+            pltpu.SemaphoreType.DMA((2,)),
+        ],
     )
-    mixed = total(lax.all_to_all(mixed.reshape(4, 64, depth), ("xh", "za"), 0, 0))
-    mixed = lax.all_to_all(mixed.astype(jnp.bfloat16).reshape(4, 16, depth), "zh", 0, 0)
+    mixed = total(lax.all_to_all(mixed.reshape(4, 64, depth), LOOP, 0, 0, axis_index_groups=NEAR))
+    mixed = lax.all_to_all(mixed.astype(jnp.bfloat16).reshape(4, 16, depth), LOOP, 0, 0, axis_index_groups=FAR)
     return total(mixed).astype(jnp.bfloat16)
 
 

time: 135 us -> 132 us (0.978)
  blocking collectives: 74.5 us -> 72 us
    all_to_all x2, blocking collectives: 35.7 us -> 33.2 us  [the longest x1 18.3 us: shards(): lax.all_to_all(mixed.astype(jnp.bfloat16).reshape(4, 16, depth), LOOP, 0,...]
where the time goes in v5:
time: 132 us
  blocking collectives  72 us (55%)
  starting transfers between devices  25.5 us (19%)
  waiting for transfers between devices  23 us (17%)
  Pallas kernels  8.09 us (6%)
  local copies, waits for them, and re-layouts  2.37 us (2%)
    all_gather x1, blocking collectives, shards(): rows = lax.all_gather(tokens, ('zh', 'za', 'zb'), axis=0, tiled=True)  38.8 us
    all_to_all x1, blocking collectives, shards(): lax.all_to_all(mixed.astype(jnp.bfloat16).reshape(4, 16, depth), LOOP, 0,...  18.3 us
    all_to_all x1, blocking collectives, shards(): lax.all_to_all(mixed.reshape(4, 64, depth), LOOP, 0, 0, axis_index_groups...  14.9 us
    all_to_all x1, waiting for transfers between devices, shards(): parts = lax.all_to_all(partial.reshape(8, 2, 32, 4 * width), NARROW, 0, 0)  10.9 us
    pallas_call x4, Pallas kernels, call(): pl.pallas_call(kernel, out_shape=jax.ShapeDtypeStruct(out_shape, jnp.bflo...  8.09 us
    all_to_all x1, starting transfers between devices, shards(): parts = lax.all_to_all(partial.reshape(8, 2, 32, 4 * width), NARROW, 0, 0)  6.07 us
    all_to_all x1, waiting for transfers between devices, shards(): lax.all_to_all(hidden.reshape(16, 32, 2 * width), (*NARROW, 'zb'), 0, 0)  5.42 us
    all_to_all x1, starting transfers between devices, shards(): lax.all_to_all(hidden.reshape(16, 32, 2 * width), (*NARROW, 'zb'), 0, 0)  5.37 us
  transfers between devices with their start and end apart: 8, of which 4 were waited for; matrix products, arithmetic and copies ran while one was open for 0% of the time, Pallas kernels for 3%

profile of v5, /device:TPU:2, one launch (start us, length us, event | category | flops | bytes accessed | tf_op | source)
XLA Modules:
  0.0 131.8 jit_solution(1056852237538635154)
XLA Ops:
  0.0 1.9 %collective-permute-start.1 = (bf16[448,1024]{1,0:T(8,128)(2,1)}, bf16[448,1024]{1,0:T(8,128)(2,1)S(1)}, u32[]{:S(2)}, u32[]{:S(2)}) collective-permute-start(bf16[448,1024]{1,0:T(8,128)(2,1)} %bitcast.9), channel_id=1, source_target_pairs={{0,8},{8,0},{1,9},{9,1},{2,10},{10,2},{3,11},{11,3},{4,12},{12,4},... | collective-permute-start | bytes 2752520 | tf_op jit(solution)/shard_map/ppermute | solution.py:122
  1.9 2.4 %collective-permute-start.2 = (bf16[448,1024]{1,0:T(8,128)(2,1)}, bf16[448,1024]{1,0:T(8,128)(2,1)S(1)}, u32[]{:S(2)}, u32[]{:S(2)}) collective-permute-start(bf16[448,1024]{1,0:T(8,128)(2,1)} %bitcast.12), channel_id=1, source_target_pairs={{0,8},{8,0},{1,9},{9,1},{2,10},{10,2},{3,11},{11,3},{4,12},{12,4},... | collective-permute-start | bytes 2752520 | tf_op jit(solution)/shard_map/ppermute | solution.py:122
  4.3 38.8 %all_gather.3.x_ref = bf16[256,1024]{1,0:T(8,128)(2,1)S(1)} all-gather(bf16[16,1024]{1,0:T(8,128)(2,1)} %param.4), channel_id=1, replica_groups=mesh['zh'=4,'za'=2,'zb'=2,'xh'=2,'core'=2,'xl'=2,'y'=4] {'zh','za','zb'}, dimensions={0}, use_global_device_ids=true | all-gather | bytes 557056 | tf_op jit(solution)/shard_map/all_gather | solution.py:124
  43.2 4.0 %collective-permute-start = (bf16[256,1024]{1,0:T(8,128)(2,1)S(1)}, bf16[256,1024]{1,0:T(8,128)(2,1)S(1)}, u32[]{:S(2)}, u32[]{:S(2)}) collective-permute-start(bf16[256,1024]{1,0:T(8,128)(2,1)S(1)} %all_gather.3.x_ref), channel_id=1, source_target_pairs={{0,16},{16,0},{1,17},{17,1},{2,18},{18,2},{3,19},{19,3},{4,20},{20... | collective-permute-start | bytes 1572872 | tf_op jit(solution)/shard_map/ppermute | solution.py:126
  47.2 0.0 collective-permute-done.1.refs_1_
  47.2 0.0 collective-permute-done.2.refs_3_
  47.2 0.0 copy-start
  47.2 1.2 copy-done
  48.4 0.0 copy-start.2
  48.4 1.2 copy-done.2
  49.6 0.0 copy-start.1
  49.6 0.0 copy-start.3
  49.6 2.2 %shard_map.46.refs_4_ = bf16[2,2,2,2,2,16,1792]{6,5,4,3,2,1,0:T(8,128)(2,1)} custom-call(s32[1]{0:T(128)} %bitcast.1.slot_ref, bf16[256,1024]{1,0:T(8,128)(2,1)S(1)} %all_gather.3.x_ref, bf16[448,1024]{1,0:T(8,128)(2,1)S(1)} %bitcast.10, bf16[448,1024]{1,0:T(8,128)(2,1)S(1)} %collective-permute-done.1.refs_1_, bf16[448,1024]{1,0:T(8,128)(2,1)S(1)} %bitcast.13, ...), custom_call_target="tpu_custom_call" | custom-call | flops 939524096 | bytes 4194306 | tf_op jit(solution)/shard_map/pallas_call | solution.py:102
  51.8 4.0 %collective-permute-done.x_ref = bf16[256,1024]{1,0:T(8,128)(2,1)S(1)} collective-permute-done((bf16[256,1024]{1,0:T(8,128)(2,1)S(1)}, bf16[256,1024]{1,0:T(8,128)(2,1)S(1)}, u32[]{:S(2)}, u32[]{:S(2)}) %collective-permute-start) | collective-permute-done | bytes 524320 | tf_op jit(solution)/shard_map/ppermute | solution.py:126
  55.7 0.0 copy-done.1
  55.7 0.0 copy-done.3
  55.7 2.2 %shard_map.47 = bf16[2,2,2,2,2,16,1792]{6,5,4,3,2,1,0:T(8,128)(2,1)} custom-call(s32[1]{0:T(128)S(6)} %sub.3.slot_ref, bf16[256,1024]{1,0:T(8,128)(2,1)S(1)} %collective-permute-done.x_ref, bf16[448,1024]{1,0:T(8,128)(2,1)S(1)} %bitcast.11, bf16[448,1024]{1,0:T(8,128)(2,1)S(1)} %collective-permute-done.1.refs_1_, ...), custom_call_target="tpu_custom_call", output_to_operand_aliasing={{}: (6, {})} | custom-call | flops 939524096 | bytes 6029314 | tf_op jit(solution)/shard_map/pallas_call | solution.py:102
  57.9 0.0 copy-start.4
  57.9 6.1 %all-to-all-start = ((bf16[8,2,32,1792]{3,2,1,0:T(8,128)(2,1)}), bf16[8,2,32,1792]{3,2,1,0:T(8,128)(2,1)S(1)}, u32[]{:S(2)}, u32[]{:S(2)}) async-start(bf16[8,2,32,1792]{3,2,1,0:T(8,128)(2,1)} %bitcast.4), calls=%async_computation | async-start | bytes 3670016 | tf_op jit(solution)/shard_map/all_to_all | solution.py:151
  64.0 0.0 copy-done.4
  64.0 1.9 %collective-permute-start.4 = (bf16[448,1024]{1,0:T(8,128)(2,1)S(1)}, bf16[448,1024]{1,0:T(8,128)(2,1)}, u32[]{:S(2)}, u32[]{:S(2)}) collective-permute-start(bf16[448,1024]{1,0:T(8,128)(2,1)S(1)} %copy-done.4), channel_id=1, source_target_pairs={{0,32},{32,0},{1,33},{33,1},{2,34},{34,2},{3,35},{35,3},{4,36},{36... | collective-permute-start | bytes 2752520 | tf_op jit(solution)/shard_map/ppermute | solution.py:149
  65.9 1.9 %collective-permute-start.3 = (bf16[448,1024]{1,0:T(8,128)(2,1)S(1)}, bf16[448,1024]{1,0:T(8,128)(2,1)}, u32[]{:S(2)}, u32[]{:S(2)}) collective-permute-start(bf16[448,1024]{1,0:T(8,128)(2,1)S(1)} %copy-done.4), channel_id=1, source_target_pairs={{0,8},{8,0},{1,9},{9,1},{2,10},{10,2},{3,11},{11,3},{4,12},{12,4},... | collective-permute-start | bytes 2752520 | tf_op jit(solution)/shard_map/ppermute | solution.py:150
  67.9 10.9 %all-to-all-done.parts_ref = bf16[8,2,32,1792]{3,2,1,0:T(8,128)(2,1)S(1)} async-done(((bf16[8,2,32,1792]{3,2,1,0:T(8,128)(2,1)}), bf16[8,2,32,1792]{3,2,1,0:T(8,128)(2,1)S(1)}, u32[]{:S(2)}, u32[]{:S(2)}) %all-to-all-start) | async-done | bytes 1835040 | tf_op jit(solution)/shard_map/all_to_all | solution.py:151
  78.8 1.2 shard_map.48
  80.0 0.0 collective-permute-done.4.refs_2_
  80.0 0.0 collective-permute-done.3.refs_1_
  80.0 5.4 %all-to-all-start.1 = ((bf16[16,32,896]{2,1,0:T(8,128)(2,1)}), bf16[16,32,896]{2,1,0:T(8,128)(2,1)S(1)}, u32[]{:S(2)}, u32[]{:S(2)}) async-start(bf16[16,32,896]{2,1,0:T(8,128)(2,1)} %bitcast.5), calls=%async_computation.1 | async-start | bytes 1835008 | tf_op jit(solution)/shard_map/all_to_all | solution.py:155
  85.4 1.9 %collective-permute-start.5 = (bf16[448,1024]{1,0:T(8,128)(2,1)}, bf16[448,1024]{1,0:T(8,128)(2,1)S(1)}, u32[]{:S(2)}, u32[]{:S(2)}) collective-permute-start(bf16[448,1024]{1,0:T(8,128)(2,1)} %collective-permute-done.4.refs_2_), channel_id=1, source_target_pairs={{0,8},{8,0},{1,9},{9,1},{2,10},{10,2},{3,11},{11,3},{4,12},{12,4},... | collective-permute-start | bytes 2752520 | tf_op jit(solution)/shard_map/ppermute | solution.py:154
  87.3 2.6 %collective-permute-done.5.refs_3_ = bf16[448,1024]{1,0:T(8,128)(2,1)S(1)} collective-permute-done((bf16[448,1024]{1,0:T(8,128)(2,1)}, bf16[448,1024]{1,0:T(8,128)(2,1)S(1)}, u32[]{:S(2)}, u32[]{:S(2)}) %collective-permute-start.5) | collective-permute-done | bytes 917536 | tf_op jit(solution)/shard_map/ppermute | solution.py:154
  89.9 5.4 %all-to-all-done.1 = bf16[16,32,896]{2,1,0:T(8,128)(2,1)S(1)} async-done(((bf16[16,32,896]{2,1,0:T(8,128)(2,1)}), bf16[16,32,896]{2,1,0:T(8,128)(2,1)S(1)}, u32[]{:S(2)}, u32[]{:S(2)}) %all-to-all-start.1) | async-done | bytes 917536 | tf_op jit(solution)/shard_map/all_to_all | solution.py:155
  95.4 2.5 %shard_map.49 = bf16[256,1024]{1,0:T(8,128)(2,1)S(1)} custom-call(s32[1]{0:T(128)} %bitcast.at_zb_ref, bf16[8,2,32,896]{3,2,1,0:T(8,128)(2,1)S(1)} %bitcast.15, bf16[448,1024]{1,0:T(8,128)(2,1)S(1)} %copy-done.4, bf16[448,1024]{1,0:T(8,128)(2,1)} %collective-permute-done.3.refs_1_, bf16[448,1024]{1,0:T(8,128)(2,1)} %collective-permute-done.4.refs_2_, ...), custom_call_target="tpu_custom_call" | custom-call | flops 939524096 | bytes 4587522 | tf_op jit(solution)/shard_map/pallas_call | solution.py:102
  97.9 14.9 %all_to_all.20 = bf16[4,64,1024]{2,1,0:T(8,128)(2,1)S(1)} all-to-all(bf16[4,64,1024]{2,1,0:T(8,128)(2,1)S(1)} %bitcast.16), channel_id=1, replica_groups={{0,448,16,464},{8,456,24,472},{32,480,48,496},{40,488,56,504},{192,256,..., dimensions={0} | all-to-all | bytes 1048576 | tf_op jit(solution)/shard_map/all_to_all | solution.py:170
  112.8 0.1 reduce_sum.24
  112.9 18.3 %all_to_all.21 = bf16[4,16,1024]{2,1,0:T(8,128)(2,1)S(1)} all-to-all(bf16[4,16,1024]{2,1,0:T(8,128)(2,1)S(1)} %bitcast.17), channel_id=1, replica_groups={{0,192,384,64},{8,200,392,72},{16,208,400,80},{24,216,408,88},{32,224,4..., dimensions={0} | all-to-all | bytes 262144 | tf_op jit(solution)/shard_map/all_to_all | solution.py:171
  131.2 0.6 reduce_sum.25
Async XLA Ops:
  0.0 47.2 %collective-permute-start.1 = (bf16[448,1024]{1,0:T(8,128)(2,1)}, bf16[448,1024]{1,0:T(8,128)(2,1)S(1)}, u32[]{:S(2)}, u32[]{:S(2)}) collective-permute-start(bf16[448,1024]{1,0:T(8,128)(2,1)} %bitcast.9), channel_id=1, source_target_pairs={{0,8},{8,0},{1,9},{9,1},{2,10},{10,2},{3,11},{11,3},{4,12},{12,4},... | collective-permute-start | bytes 2752520 | tf_op jit(solution)/shard_map/ppermute | solution.py:122
  1.9 45.3 %collective-permute-start.2 = (bf16[448,1024]{1,0:T(8,128)(2,1)}, bf16[448,1024]{1,0:T(8,128)(2,1)S(1)}, u32[]{:S(2)}, u32[]{:S(2)}) collective-permute-start(bf16[448,1024]{1,0:T(8,128)(2,1)} %bitcast.12), channel_id=1, source_target_pairs={{0,8},{8,0},{1,9},{9,1},{2,10},{10,2},{3,11},{11,3},{4,12},{12,4},... | collective-permute-start | bytes 2752520 | tf_op jit(solution)/shard_map/ppermute | solution.py:122
  43.2 12.6 %collective-permute-start = (bf16[256,1024]{1,0:T(8,128)(2,1)S(1)}, bf16[256,1024]{1,0:T(8,128)(2,1)S(1)}, u32[]{:S(2)}, u32[]{:S(2)}) collective-permute-start(bf16[256,1024]{1,0:T(8,128)(2,1)S(1)} %all_gather.3.x_ref), channel_id=1, source_target_pairs={{0,16},{16,0},{1,17},{17,1},{2,18},{18,2},{3,19},{19,3},{4,20},{20... | collective-permute-start | bytes 1572872 | tf_op jit(solution)/shard_map/ppermute | solution.py:126
  47.2 1.2 copy-start
  48.4 1.2 copy-start.2
  49.6 6.2 %copy-start.1 = (bf16[1024,448]{0,1:T(8,128)(2,1)S(1)}, bf16[1024,448]{0,1:T(8,128)(2,1)}, u32[]{:S(2)}) copy-start(bf16[1024,448]{0,1:T(8,128)(2,1)} %param.5) | copy-start | bytes 2752516
  49.6 6.2 %copy-start.3 = (bf16[1024,448]{0,1:T(8,128)(2,1)S(1)}, bf16[1024,448]{0,1:T(8,128)(2,1)}, u32[]{:S(2)}) copy-start(bf16[1024,448]{0,1:T(8,128)(2,1)} %param.6) | copy-start | bytes 2752516
  57.9 6.1 %copy-start.4 = (bf16[448,1024]{1,0:T(8,128)(2,1)S(1)}, bf16[448,1024]{1,0:T(8,128)(2,1)}, u32[]{:S(2)}) copy-start(bf16[448,1024]{1,0:T(8,128)(2,1)} %refs_0_) | copy-start | bytes 2752516
  57.9 20.9 %all-to-all-start = ((bf16[8,2,32,1792]{3,2,1,0:T(8,128)(2,1)}), bf16[8,2,32,1792]{3,2,1,0:T(8,128)(2,1)S(1)}, u32[]{:S(2)}, u32[]{:S(2)}) async-start(bf16[8,2,32,1792]{3,2,1,0:T(8,128)(2,1)} %bitcast.4), calls=%async_computation | async-start | bytes 3670016 | tf_op jit(solution)/shard_map/all_to_all | solution.py:151
  64.0 16.0 %collective-permute-start.4 = (bf16[448,1024]{1,0:T(8,128)(2,1)S(1)}, bf16[448,1024]{1,0:T(8,128)(2,1)}, u32[]{:S(2)}, u32[]{:S(2)}) collective-permute-start(bf16[448,1024]{1,0:T(8,128)(2,1)S(1)} %copy-done.4), channel_id=1, source_target_pairs={{0,32},{32,0},{1,33},{33,1},{2,34},{34,2},{3,35},{35,3},{4,36},{36... | collective-permute-start | bytes 2752520 | tf_op jit(solution)/shard_map/ppermute | solution.py:149
  65.9 14.1 %collective-permute-start.3 = (bf16[448,1024]{1,0:T(8,128)(2,1)S(1)}, bf16[448,1024]{1,0:T(8,128)(2,1)}, u32[]{:S(2)}, u32[]{:S(2)}) collective-permute-start(bf16[448,1024]{1,0:T(8,128)(2,1)S(1)} %copy-done.4), channel_id=1, source_target_pairs={{0,8},{8,0},{1,9},{9,1},{2,10},{10,2},{3,11},{11,3},{4,12},{12,4},... | collective-permute-start | bytes 2752520 | tf_op jit(solution)/shard_map/ppermute | solution.py:150
  80.0 15.4 %all-to-all-start.1 = ((bf16[16,32,896]{2,1,0:T(8,128)(2,1)}), bf16[16,32,896]{2,1,0:T(8,128)(2,1)S(1)}, u32[]{:S(2)}, u32[]{:S(2)}) async-start(bf16[16,32,896]{2,1,0:T(8,128)(2,1)} %bitcast.5), calls=%async_computation.1 | async-start | bytes 1835008 | tf_op jit(solution)/shard_map/all_to_all | solution.py:155
  85.4 4.6 %collective-permute-start.5 = (bf16[448,1024]{1,0:T(8,128)(2,1)}, bf16[448,1024]{1,0:T(8,128)(2,1)S(1)}, u32[]{:S(2)}, u32[]{:S(2)}) collective-permute-start(bf16[448,1024]{1,0:T(8,128)(2,1)} %collective-permute-done.4.refs_2_), channel_id=1, source_target_pairs={{0,8},{8,0},{1,9},{9,1},{2,10},{10,2},{3,11},{11,3},{4,12},{12,4},... | collective-permute-start | bytes 2752520 | tf_op jit(solution)/shard_map/ppermute | solution.py:154

commit v6 on v5

--- a/solution.py
+++ b/solution.py
@@ -13,11 +13,16 @@
 
 
 def loop_at(pair, zb, xh, core):
-    return pair * 8 + zb * 4 + xh * 2 + core
+    return (pair + core) % 8 * 8 + zb * 4 + xh * 2 + core
 
 
+ALONG_Z = [
+    [loop_at(pair, zb, xh, core) for pair in range(8) for zb in range(2)]
+    for xh in range(2)
+    for core in range(2)
+]
 NEAR = [
-    [loop_at(group[at], zb, xh, core) for xh in range(2) for group in GROUPS]
+    [loop_at(group[at], zb, xh, core) for group in GROUPS for xh in range(2)]
     for at in range(4)
     for zb in range(2)
     for core in range(2)
@@ -59,7 +64,7 @@
             copies.append(
                 pltpu.make_async_copy(
                     block_ref.at[..., half],
-                    out_ref.at[slot_ref[0], :, :, :, :, :, half],
+                    out_ref.at[:, slot_ref[0], :, :, :, :, half],
                     sems.at[i // 2],
                 )
             )
@@ -121,7 +126,7 @@
     width = gate.shape[0]
     weights = [gate, lax.ppermute(gate, "core", SWAP), up, lax.ppermute(up, "core", SWAP)]
 
-    rows = lax.all_gather(tokens, ("zh", "za", "zb"), axis=0, tiled=True)
+    rows = lax.all_gather(tokens, LOOP, axis=0, tiled=True, axis_index_groups=ALONG_Z)
     n_rows = rows.shape[0]
     other_rows = lax.ppermute(rows, "xh", SWAP)
     flops = 8 * n_rows * depth * width

time: 132 us -> 133 us (level)
  no operation moved by 1% of the time
where the time goes in v6:
time: 133 us; the launch traced here: 132 us
  blocking collectives  72.1 us (54%)
  starting transfers between devices  25.5 us (19%)
  waiting for transfers between devices  22.7 us (17%)
  Pallas kernels  8.61 us (6%)
  local copies, waits for them, and re-layouts  2.37 us (2%)
    all_gather x1, blocking collectives, shards(): lax.all_gather(tokens, LOOP, axis=0, tiled=True, axis_index_groups=ALONG_Z)  38.8 us
    all_to_all x1, blocking collectives, shards(): lax.all_to_all(mixed.astype(jnp.bfloat16).reshape(4, 16, depth), LOOP, 0,...  18.3 us
    all_to_all x1, blocking collectives, shards(): lax.all_to_all(mixed.reshape(4, 64, depth), LOOP, 0, 0, axis_index_groups...  15 us
    all_to_all x1, waiting for transfers between devices, shards(): parts = lax.all_to_all(partial.reshape(8, 2, 32, 4 * width), NARROW, 0, 0)  10.9 us
    pallas_call x4, Pallas kernels, call(): pl.pallas_call(kernel, out_shape=jax.ShapeDtypeStruct(out_shape, jnp.bflo...  8.61 us
    all_to_all x1, starting transfers between devices, shards(): parts = lax.all_to_all(partial.reshape(8, 2, 32, 4 * width), NARROW, 0, 0)  6.08 us
    all_to_all x1, waiting for transfers between devices, shards(): lax.all_to_all(hidden.reshape(16, 32, 2 * width), (*NARROW, 'zb'), 0, 0)  5.42 us
    all_to_all x1, starting transfers between devices, shards(): lax.all_to_all(hidden.reshape(16, 32, 2 * width), (*NARROW, 'zb'), 0, 0)  5.37 us
  transfers between devices with their start and end apart: 8, of which 4 were waited for; matrix products, arithmetic and copies ran while one was open for 0% of the time, Pallas kernels for 3%

profile of v6, /device:TPU:2, one launch (start us, length us, event | category | flops | bytes accessed | tf_op | source)
XLA Modules:
  0.0 132.1 jit_solution(2314069371481512856)
XLA Ops:
  0.0 1.9 %collective-permute-start.1 = (bf16[448,1024]{1,0:T(8,128)(2,1)}, bf16[448,1024]{1,0:T(8,128)(2,1)S(1)}, u32[]{:S(2)}, u32[]{:S(2)}) collective-permute-start(bf16[448,1024]{1,0:T(8,128)(2,1)} %bitcast.9), channel_id=1, source_target_pairs={{0,8},{8,0},{1,9},{9,1},{2,10},{10,2},{3,11},{11,3},{4,12},{12,4},... | collective-permute-start | bytes 2752520 | tf_op jit(solution)/shard_map/ppermute | solution.py:127
  1.9 2.4 %collective-permute-start.2 = (bf16[448,1024]{1,0:T(8,128)(2,1)}, bf16[448,1024]{1,0:T(8,128)(2,1)S(1)}, u32[]{:S(2)}, u32[]{:S(2)}) collective-permute-start(bf16[448,1024]{1,0:T(8,128)(2,1)} %bitcast.12), channel_id=1, source_target_pairs={{0,8},{8,0},{1,9},{9,1},{2,10},{10,2},{3,11},{11,3},{4,12},{12,4},... | collective-permute-start | bytes 2752520 | tf_op jit(solution)/shard_map/ppermute | solution.py:127
  4.3 38.8 %all_gather.3.x_ref = bf16[256,1024]{1,0:T(8,128)(2,1)S(1)} all-gather(bf16[16,1024]{1,0:T(8,128)(2,1)} %param.4), channel_id=1, replica_groups={{0,32,64,96,128,160,192,224,256,288,320,352,384,416,448,480},{72,104,13..., dimensions={0}, use_global_device_ids=true | all-gather | bytes 557056 | tf_op jit(solution)/shard_map/all_gather | solution.py:129
  43.2 4.0 %collective-permute-start = (bf16[256,1024]{1,0:T(8,128)(2,1)S(1)}, bf16[256,1024]{1,0:T(8,128)(2,1)S(1)}, u32[]{:S(2)}, u32[]{:S(2)}) collective-permute-start(bf16[256,1024]{1,0:T(8,128)(2,1)S(1)} %all_gather.3.x_ref), channel_id=1, source_target_pairs={{0,16},{16,0},{1,17},{17,1},{2,18},{18,2},{3,19},{19,3},{4,20},{20... | collective-permute-start | bytes 1572872 | tf_op jit(solution)/shard_map/ppermute | solution.py:131
  47.2 0.0 collective-permute-done.1.refs_1_
  47.2 0.0 collective-permute-done.2.refs_3_
  47.2 0.0 copy-start
  47.2 1.2 copy-done
  48.4 0.0 copy-start.2
  48.4 1.2 copy-done.2
  49.6 0.0 copy-start.1
  49.6 0.0 copy-start.3
  49.6 2.5 %shard_map.46.refs_4_ = bf16[2,2,2,2,2,16,1792]{6,5,4,3,2,1,0:T(8,128)(2,1)} custom-call(s32[1]{0:T(128)} %bitcast.1.slot_ref, bf16[256,1024]{1,0:T(8,128)(2,1)S(1)} %all_gather.3.x_ref, bf16[448,1024]{1,0:T(8,128)(2,1)S(1)} %bitcast.10, bf16[448,1024]{1,0:T(8,128)(2,1)S(1)} %collective-permute-done.1.refs_1_, bf16[448,1024]{1,0:T(8,128)(2,1)S(1)} %bitcast.13, ...), custom_call_target="tpu_custom_call" | custom-call | flops 939524096 | bytes 4194306 | tf_op jit(solution)/shard_map/pallas_call | solution.py:107
  52.1 3.7 %collective-permute-done.x_ref = bf16[256,1024]{1,0:T(8,128)(2,1)S(1)} collective-permute-done((bf16[256,1024]{1,0:T(8,128)(2,1)S(1)}, bf16[256,1024]{1,0:T(8,128)(2,1)S(1)}, u32[]{:S(2)}, u32[]{:S(2)}) %collective-permute-start) | collective-permute-done | bytes 524320 | tf_op jit(solution)/shard_map/ppermute | solution.py:131
  55.7 0.0 copy-done.1
  55.7 0.0 copy-done.3
  55.7 2.4 %shard_map.47 = bf16[2,2,2,2,2,16,1792]{6,5,4,3,2,1,0:T(8,128)(2,1)} custom-call(s32[1]{0:T(128)S(6)} %sub.3.slot_ref, bf16[256,1024]{1,0:T(8,128)(2,1)S(1)} %collective-permute-done.x_ref, bf16[448,1024]{1,0:T(8,128)(2,1)S(1)} %bitcast.11, bf16[448,1024]{1,0:T(8,128)(2,1)S(1)} %collective-permute-done.1.refs_1_, ...), custom_call_target="tpu_custom_call", output_to_operand_aliasing={{}: (6, {})} | custom-call | flops 939524096 | bytes 6029314 | tf_op jit(solution)/shard_map/pallas_call | solution.py:107
  58.2 0.0 copy-start.4
  58.2 6.1 %all-to-all-start = ((bf16[8,2,32,1792]{3,2,1,0:T(8,128)(2,1)}), bf16[8,2,32,1792]{3,2,1,0:T(8,128)(2,1)S(1)}, u32[]{:S(2)}, u32[]{:S(2)}) async-start(bf16[8,2,32,1792]{3,2,1,0:T(8,128)(2,1)} %bitcast.4), calls=%async_computation | async-start | bytes 3670016 | tf_op jit(solution)/shard_map/all_to_all | solution.py:156
  64.2 0.0 copy-done.4
  64.2 1.9 %collective-permute-start.4 = (bf16[448,1024]{1,0:T(8,128)(2,1)S(1)}, bf16[448,1024]{1,0:T(8,128)(2,1)}, u32[]{:S(2)}, u32[]{:S(2)}) collective-permute-start(bf16[448,1024]{1,0:T(8,128)(2,1)S(1)} %copy-done.4), channel_id=1, source_target_pairs={{0,32},{32,0},{1,33},{33,1},{2,34},{34,2},{3,35},{35,3},{4,36},{36... | collective-permute-start | bytes 2752520 | tf_op jit(solution)/shard_map/ppermute | solution.py:154
  66.2 1.9 %collective-permute-start.3 = (bf16[448,1024]{1,0:T(8,128)(2,1)S(1)}, bf16[448,1024]{1,0:T(8,128)(2,1)}, u32[]{:S(2)}, u32[]{:S(2)}) collective-permute-start(bf16[448,1024]{1,0:T(8,128)(2,1)S(1)} %copy-done.4), channel_id=1, source_target_pairs={{0,8},{8,0},{1,9},{9,1},{2,10},{10,2},{3,11},{11,3},{4,12},{12,4},... | collective-permute-start | bytes 2752520 | tf_op jit(solution)/shard_map/ppermute | solution.py:155
  68.1 10.9 %all-to-all-done.parts_ref = bf16[8,2,32,1792]{3,2,1,0:T(8,128)(2,1)S(1)} async-done(((bf16[8,2,32,1792]{3,2,1,0:T(8,128)(2,1)}), bf16[8,2,32,1792]{3,2,1,0:T(8,128)(2,1)S(1)}, u32[]{:S(2)}, u32[]{:S(2)}) %all-to-all-start) | async-done | bytes 1835040 | tf_op jit(solution)/shard_map/all_to_all | solution.py:156
  79.0 1.2 shard_map.48
  80.2 0.0 collective-permute-done.4.refs_2_
  80.2 0.0 collective-permute-done.3.refs_1_
  80.2 5.4 %all-to-all-start.1 = ((bf16[16,32,896]{2,1,0:T(8,128)(2,1)}), bf16[16,32,896]{2,1,0:T(8,128)(2,1)S(1)}, u32[]{:S(2)}, u32[]{:S(2)}) async-start(bf16[16,32,896]{2,1,0:T(8,128)(2,1)} %bitcast.5), calls=%async_computation.1 | async-start | bytes 1835008 | tf_op jit(solution)/shard_map/all_to_all | solution.py:160
  85.6 1.9 %collective-permute-start.5 = (bf16[448,1024]{1,0:T(8,128)(2,1)}, bf16[448,1024]{1,0:T(8,128)(2,1)S(1)}, u32[]{:S(2)}, u32[]{:S(2)}) collective-permute-start(bf16[448,1024]{1,0:T(8,128)(2,1)} %collective-permute-done.4.refs_2_), channel_id=1, source_target_pairs={{0,8},{8,0},{1,9},{9,1},{2,10},{10,2},{3,11},{11,3},{4,12},{12,4},... | collective-permute-start | bytes 2752520 | tf_op jit(solution)/shard_map/ppermute | solution.py:159
  87.5 2.6 %collective-permute-done.5.refs_3_ = bf16[448,1024]{1,0:T(8,128)(2,1)S(1)} collective-permute-done((bf16[448,1024]{1,0:T(8,128)(2,1)}, bf16[448,1024]{1,0:T(8,128)(2,1)S(1)}, u32[]{:S(2)}, u32[]{:S(2)}) %collective-permute-start.5) | collective-permute-done | bytes 917536 | tf_op jit(solution)/shard_map/ppermute | solution.py:159
  90.2 5.4 %all-to-all-done.1 = bf16[16,32,896]{2,1,0:T(8,128)(2,1)S(1)} async-done(((bf16[16,32,896]{2,1,0:T(8,128)(2,1)}), bf16[16,32,896]{2,1,0:T(8,128)(2,1)S(1)}, u32[]{:S(2)}, u32[]{:S(2)}) %all-to-all-start.1) | async-done | bytes 917536 | tf_op jit(solution)/shard_map/all_to_all | solution.py:160
  95.6 2.5 %shard_map.49 = bf16[256,1024]{1,0:T(8,128)(2,1)S(1)} custom-call(s32[1]{0:T(128)} %bitcast.at_zb_ref, bf16[8,2,32,896]{3,2,1,0:T(8,128)(2,1)S(1)} %bitcast.15, bf16[448,1024]{1,0:T(8,128)(2,1)S(1)} %copy-done.4, bf16[448,1024]{1,0:T(8,128)(2,1)} %collective-permute-done.3.refs_1_, bf16[448,1024]{1,0:T(8,128)(2,1)} %collective-permute-done.4.refs_2_, ...), custom_call_target="tpu_custom_call" | custom-call | flops 939524096 | bytes 4587522 | tf_op jit(solution)/shard_map/pallas_call | solution.py:107
  98.1 15.0 %all_to_all.20 = bf16[4,64,1024]{2,1,0:T(8,128)(2,1)S(1)} all-to-all(bf16[4,64,1024]{2,1,0:T(8,128)(2,1)S(1)} %bitcast.16), channel_id=1, replica_groups={{0,16,448,464},{72,88,8,24},{32,48,480,496},{104,120,40,56},{192,208,25..., dimensions={0} | all-to-all | bytes 1048576 | tf_op jit(solution)/shard_map/all_to_all | solution.py:175
  113.1 0.1 reduce_sum.24
  113.2 18.3 %all_to_all.21 = bf16[4,16,1024]{2,1,0:T(8,128)(2,1)S(1)} all-to-all(bf16[4,16,1024]{2,1,0:T(8,128)(2,1)S(1)} %bitcast.17), channel_id=1, replica_groups={{0,192,384,64},{72,264,456,136},{16,208,400,80},{88,280,472,152},{32,22..., dimensions={0} | all-to-all | bytes 262144 | tf_op jit(solution)/shard_map/all_to_all | solution.py:176
  131.5 0.6 reduce_sum.25
Async XLA Ops:
  0.0 47.2 %collective-permute-start.1 = (bf16[448,1024]{1,0:T(8,128)(2,1)}, bf16[448,1024]{1,0:T(8,128)(2,1)S(1)}, u32[]{:S(2)}, u32[]{:S(2)}) collective-permute-start(bf16[448,1024]{1,0:T(8,128)(2,1)} %bitcast.9), channel_id=1, source_target_pairs={{0,8},{8,0},{1,9},{9,1},{2,10},{10,2},{3,11},{11,3},{4,12},{12,4},... | collective-permute-start | bytes 2752520 | tf_op jit(solution)/shard_map/ppermute | solution.py:127
  1.9 45.3 %collective-permute-start.2 = (bf16[448,1024]{1,0:T(8,128)(2,1)}, bf16[448,1024]{1,0:T(8,128)(2,1)S(1)}, u32[]{:S(2)}, u32[]{:S(2)}) collective-permute-start(bf16[448,1024]{1,0:T(8,128)(2,1)} %bitcast.12), channel_id=1, source_target_pairs={{0,8},{8,0},{1,9},{9,1},{2,10},{10,2},{3,11},{11,3},{4,12},{12,4},... | collective-permute-start | bytes 2752520 | tf_op jit(solution)/shard_map/ppermute | solution.py:127
  43.2 12.6 %collective-permute-start = (bf16[256,1024]{1,0:T(8,128)(2,1)S(1)}, bf16[256,1024]{1,0:T(8,128)(2,1)S(1)}, u32[]{:S(2)}, u32[]{:S(2)}) collective-permute-start(bf16[256,1024]{1,0:T(8,128)(2,1)S(1)} %all_gather.3.x_ref), channel_id=1, source_target_pairs={{0,16},{16,0},{1,17},{17,1},{2,18},{18,2},{3,19},{19,3},{4,20},{20... | collective-permute-start | bytes 1572872 | tf_op jit(solution)/shard_map/ppermute | solution.py:131
  47.2 1.2 copy-start
  48.4 1.2 copy-start.2
  49.6 6.2 %copy-start.1 = (bf16[1024,448]{0,1:T(8,128)(2,1)S(1)}, bf16[1024,448]{0,1:T(8,128)(2,1)}, u32[]{:S(2)}) copy-start(bf16[1024,448]{0,1:T(8,128)(2,1)} %param.5) | copy-start | bytes 2752516
  49.6 6.2 %copy-start.3 = (bf16[1024,448]{0,1:T(8,128)(2,1)S(1)}, bf16[1024,448]{0,1:T(8,128)(2,1)}, u32[]{:S(2)}) copy-start(bf16[1024,448]{0,1:T(8,128)(2,1)} %param.6) | copy-start | bytes 2752516
  58.2 6.1 %copy-start.4 = (bf16[448,1024]{1,0:T(8,128)(2,1)S(1)}, bf16[448,1024]{1,0:T(8,128)(2,1)}, u32[]{:S(2)}) copy-start(bf16[448,1024]{1,0:T(8,128)(2,1)} %refs_0_) | copy-start | bytes 2752516
  58.2 20.9 %all-to-all-start = ((bf16[8,2,32,1792]{3,2,1,0:T(8,128)(2,1)}), bf16[8,2,32,1792]{3,2,1,0:T(8,128)(2,1)S(1)}, u32[]{:S(2)}, u32[]{:S(2)}) async-start(bf16[8,2,32,1792]{3,2,1,0:T(8,128)(2,1)} %bitcast.4), calls=%async_computation | async-start | bytes 3670016 | tf_op jit(solution)/shard_map/all_to_all | solution.py:156
  64.2 16.0 %collective-permute-start.4 = (bf16[448,1024]{1,0:T(8,128)(2,1)S(1)}, bf16[448,1024]{1,0:T(8,128)(2,1)}, u32[]{:S(2)}, u32[]{:S(2)}) collective-permute-start(bf16[448,1024]{1,0:T(8,128)(2,1)S(1)} %copy-done.4), channel_id=1, source_target_pairs={{0,32},{32,0},{1,33},{33,1},{2,34},{34,2},{3,35},{35,3},{4,36},{36... | collective-permute-start | bytes 2752520 | tf_op jit(solution)/shard_map/ppermute | solution.py:154
  66.2 14.1 %collective-permute-start.3 = (bf16[448,1024]{1,0:T(8,128)(2,1)S(1)}, bf16[448,1024]{1,0:T(8,128)(2,1)}, u32[]{:S(2)}, u32[]{:S(2)}) collective-permute-start(bf16[448,1024]{1,0:T(8,128)(2,1)S(1)} %copy-done.4), channel_id=1, source_target_pairs={{0,8},{8,0},{1,9},{9,1},{2,10},{10,2},{3,11},{11,3},{4,12},{12,4},... | collective-permute-start | bytes 2752520 | tf_op jit(solution)/shard_map/ppermute | solution.py:155
  80.2 15.4 %all-to-all-start.1 = ((bf16[16,32,896]{2,1,0:T(8,128)(2,1)}), bf16[16,32,896]{2,1,0:T(8,128)(2,1)S(1)}, u32[]{:S(2)}, u32[]{:S(2)}) async-start(bf16[16,32,896]{2,1,0:T(8,128)(2,1)} %bitcast.5), calls=%async_computation.1 | async-start | bytes 1835008 | tf_op jit(solution)/shard_map/all_to_all | solution.py:160
  85.6 4.6 %collective-permute-start.5 = (bf16[448,1024]{1,0:T(8,128)(2,1)}, bf16[448,1024]{1,0:T(8,128)(2,1)S(1)}, u32[]{:S(2)}, u32[]{:S(2)}) collective-permute-start(bf16[448,1024]{1,0:T(8,128)(2,1)} %collective-permute-done.4.refs_2_), channel_id=1, source_target_pairs={{0,8},{8,0},{1,9},{9,1},{2,10},{10,2},{3,11},{11,3},{4,12},{12,4},... | collective-permute-start | bytes 2752520 | tf_op jit(solution)/shard_map/ppermute | solution.py:159

commit v7 on v5

--- a/solution.py
+++ b/solution.py
@@ -7,6 +7,7 @@
 
 AXES = ("zh", "za", "zb", "xh", "core", "xl", "y")
 NARROW = ("xl", "y")
+FLIPPED = ("y", "xl")
 SWAP = [(0, 1), (1, 0)]
 LOOP = ("zh", "za", "zb", "xh", "core")
 GROUPS = ((0, 3, 6, 1), (7, 4, 5, 2))
@@ -148,11 +149,11 @@
     down_weight, partial = lax.optimization_barrier((down_weight, partial))
     down_far = lax.ppermute(down_weight, "zb", SWAP)
     down_core = lax.ppermute(down_weight, "core", SWAP)
-    parts = lax.all_to_all(partial.reshape(8, 2, 32, 4 * width), NARROW, 0, 0)
+    parts = lax.all_to_all(partial.reshape(8, 2, 32, 4 * width), FLIPPED, 0, 0)
     hidden = call(hidden_kernel, [VMEM], (8, 2, 32, 2 * width), 16 * 64 * 4 * width, parts)
     hidden, down_core, down_far = lax.optimization_barrier((hidden, down_core, down_far))
     downs = [down_weight, down_core, down_far, lax.ppermute(down_far, "core", SWAP)]
-    hidden = lax.all_to_all(hidden.reshape(16, 32, 2 * width), (*NARROW, "zb"), 0, 0)
+    hidden = lax.all_to_all(hidden.reshape(16, 32, 2 * width), (*FLIPPED, "zb"), 0, 0)
     hidden = hidden.reshape(8, 2, 32, 2 * width)
     mixed = call(
         down_kernel,

time: 132 us -> 133 us (level)
  the two profiles are of different devices: /device:TPU:2 before, /device:TPU:16 now
where the time goes in v7:
time: 133 us; the launch traced here: 132 us
  blocking collectives  73.4 us (55%)
  starting transfers between devices  27.1 us (20%)
  waiting for transfers between devices  20.2 us (15%)
  Pallas kernels  8.09 us (6%)
  local copies, waits for them, and re-layouts  2.37 us (2%)
    all_gather x1, blocking collectives, shards(): rows = lax.all_gather(tokens, ('zh', 'za', 'zb'), axis=0, tiled=True)  38.8 us
    all_to_all x1, blocking collectives, shards(): lax.all_to_all(mixed.astype(jnp.bfloat16).reshape(4, 16, depth), LOOP, 0,...  19.1 us
    all_to_all x1, blocking collectives, shards(): lax.all_to_all(mixed.reshape(4, 64, depth), LOOP, 0, 0, axis_index_groups...  15.5 us
    all_to_all x1, waiting for transfers between devices, shards(): parts = lax.all_to_all(partial.reshape(8, 2, 32, 4 * width), FLIPPED, 0, 0)  10.2 us
    pallas_call x4, Pallas kernels, call(): pl.pallas_call(kernel, out_shape=jax.ShapeDtypeStruct(out_shape, jnp.bflo...  8.09 us
    all_to_all x1, starting transfers between devices, shards(): lax.all_to_all(hidden.reshape(16, 32, 2 * width), (*FLIPPED, 'zb'), 0, 0)  6.23 us
    all_to_all x1, starting transfers between devices, shards(): parts = lax.all_to_all(partial.reshape(8, 2, 32, 4 * width), FLIPPED, 0, 0)  5.87 us
    ppermute x1, starting transfers between devices, shards(): other_rows = lax.ppermute(rows, 'xh', SWAP)  4.92 us
  transfers between devices with their start and end apart: 8, of which 5 were waited for; matrix products, arithmetic and copies ran while one was open for 0% of the time, Pallas kernels for 3%

profile of v7, /device:TPU:16, one launch (start us, length us, event | category | flops | bytes accessed | tf_op | source)
XLA Modules:
  0.0 131.9 jit_solution(4546551520758438509)
XLA Ops:
  0.0 1.9 %collective-permute-start.1 = (bf16[448,1024]{1,0:T(8,128)(2,1)}, bf16[448,1024]{1,0:T(8,128)(2,1)S(1)}, u32[]{:S(2)}, u32[]{:S(2)}) collective-permute-start(bf16[448,1024]{1,0:T(8,128)(2,1)} %bitcast.9), channel_id=1, source_target_pairs={{0,8},{8,0},{1,9},{9,1},{2,10},{10,2},{3,11},{11,3},{4,12},{12,4},... | collective-permute-start | bytes 2752520 | tf_op jit(solution)/shard_map/ppermute | solution.py:123
  1.9 2.4 %collective-permute-start.2 = (bf16[448,1024]{1,0:T(8,128)(2,1)}, bf16[448,1024]{1,0:T(8,128)(2,1)S(1)}, u32[]{:S(2)}, u32[]{:S(2)}) collective-permute-start(bf16[448,1024]{1,0:T(8,128)(2,1)} %bitcast.12), channel_id=1, source_target_pairs={{0,8},{8,0},{1,9},{9,1},{2,10},{10,2},{3,11},{11,3},{4,12},{12,4},... | collective-permute-start | bytes 2752520 | tf_op jit(solution)/shard_map/ppermute | solution.py:123
  4.3 38.8 %all_gather.3.x_ref = bf16[256,1024]{1,0:T(8,128)(2,1)S(1)} all-gather(bf16[16,1024]{1,0:T(8,128)(2,1)} %param.4), channel_id=1, replica_groups=mesh['zh'=4,'za'=2,'zb'=2,'xh'=2,'core'=2,'xl'=2,'y'=4] {'zh','za','zb'}, dimensions={0}, use_global_device_ids=true | all-gather | bytes 557056 | tf_op jit(solution)/shard_map/all_gather | solution.py:125
  43.2 4.9 %collective-permute-start = (bf16[256,1024]{1,0:T(8,128)(2,1)S(1)}, bf16[256,1024]{1,0:T(8,128)(2,1)S(1)}, u32[]{:S(2)}, u32[]{:S(2)}) collective-permute-start(bf16[256,1024]{1,0:T(8,128)(2,1)S(1)} %all_gather.3.x_ref), channel_id=1, source_target_pairs={{0,16},{16,0},{1,17},{17,1},{2,18},{18,2},{3,19},{19,3},{4,20},{20... | collective-permute-start | bytes 1572872 | tf_op jit(solution)/shard_map/ppermute | solution.py:127
  48.1 0.0 collective-permute-done.1.refs_1_
  48.1 0.0 collective-permute-done.2.refs_3_
  48.1 0.0 copy-start
  48.1 1.2 copy-done
  49.3 0.0 copy-start.2
  49.3 1.2 copy-done.2
  50.5 0.0 copy-start.1
  50.5 0.0 copy-start.3
  50.5 2.2 %shard_map.46.refs_4_ = bf16[2,2,2,2,2,16,1792]{6,5,4,3,2,1,0:T(8,128)(2,1)} custom-call(s32[1]{0:T(128)} %bitcast.1.slot_ref, bf16[256,1024]{1,0:T(8,128)(2,1)S(1)} %all_gather.3.x_ref, bf16[448,1024]{1,0:T(8,128)(2,1)S(1)} %bitcast.10, bf16[448,1024]{1,0:T(8,128)(2,1)S(1)} %collective-permute-done.1.refs_1_, bf16[448,1024]{1,0:T(8,128)(2,1)S(1)} %bitcast.13, ...), custom_call_target="tpu_custom_call" | custom-call | flops 939524096 | bytes 4194306 | tf_op jit(solution)/shard_map/pallas_call | solution.py:103
  52.7 3.1 %collective-permute-done.x_ref = bf16[256,1024]{1,0:T(8,128)(2,1)S(1)} collective-permute-done((bf16[256,1024]{1,0:T(8,128)(2,1)S(1)}, bf16[256,1024]{1,0:T(8,128)(2,1)S(1)}, u32[]{:S(2)}, u32[]{:S(2)}) %collective-permute-start) | collective-permute-done | bytes 524320 | tf_op jit(solution)/shard_map/ppermute | solution.py:127
  55.7 0.0 copy-done.1
  55.7 0.0 copy-done.3
  55.7 2.2 %shard_map.47 = bf16[2,2,2,2,2,16,1792]{6,5,4,3,2,1,0:T(8,128)(2,1)} custom-call(s32[1]{0:T(128)S(6)} %sub.3.slot_ref, bf16[256,1024]{1,0:T(8,128)(2,1)S(1)} %collective-permute-done.x_ref, bf16[448,1024]{1,0:T(8,128)(2,1)S(1)} %bitcast.11, bf16[448,1024]{1,0:T(8,128)(2,1)S(1)} %collective-permute-done.1.refs_1_, ...), custom_call_target="tpu_custom_call", output_to_operand_aliasing={{}: (6, {})} | custom-call | flops 939524096 | bytes 6029314 | tf_op jit(solution)/shard_map/pallas_call | solution.py:103
  57.9 0.0 copy-start.4
  57.9 5.9 %all-to-all-start = ((bf16[8,2,32,1792]{3,2,1,0:T(8,128)(2,1)}), bf16[8,2,32,1792]{3,2,1,0:T(8,128)(2,1)S(1)}, u32[]{:S(2)}, u32[]{:S(2)}) async-start(bf16[8,2,32,1792]{3,2,1,0:T(8,128)(2,1)} %bitcast.4), calls=%async_computation | async-start | bytes 3670016 | tf_op jit(solution)/shard_map/all_to_all | solution.py:152
  63.8 0.0 copy-done.4
  63.8 1.9 %collective-permute-start.4 = (bf16[448,1024]{1,0:T(8,128)(2,1)S(1)}, bf16[448,1024]{1,0:T(8,128)(2,1)}, u32[]{:S(2)}, u32[]{:S(2)}) collective-permute-start(bf16[448,1024]{1,0:T(8,128)(2,1)S(1)} %copy-done.4), channel_id=1, source_target_pairs={{0,32},{32,0},{1,33},{33,1},{2,34},{34,2},{3,35},{35,3},{4,36},{36... | collective-permute-start | bytes 2752520 | tf_op jit(solution)/shard_map/ppermute | solution.py:150
  65.7 1.9 %collective-permute-start.3 = (bf16[448,1024]{1,0:T(8,128)(2,1)S(1)}, bf16[448,1024]{1,0:T(8,128)(2,1)}, u32[]{:S(2)}, u32[]{:S(2)}) collective-permute-start(bf16[448,1024]{1,0:T(8,128)(2,1)S(1)} %copy-done.4), channel_id=1, source_target_pairs={{0,8},{8,0},{1,9},{9,1},{2,10},{10,2},{3,11},{11,3},{4,12},{12,4},... | collective-permute-start | bytes 2752520 | tf_op jit(solution)/shard_map/ppermute | solution.py:151
  67.7 10.2 %all-to-all-done.parts_ref = bf16[8,2,32,1792]{3,2,1,0:T(8,128)(2,1)S(1)} async-done(((bf16[8,2,32,1792]{3,2,1,0:T(8,128)(2,1)}), bf16[8,2,32,1792]{3,2,1,0:T(8,128)(2,1)S(1)}, u32[]{:S(2)}, u32[]{:S(2)}) %all-to-all-start) | async-done | bytes 1835040 | tf_op jit(solution)/shard_map/all_to_all | solution.py:152
  77.9 1.2 shard_map.48
  79.1 0.4 collective-permute-done.4.refs_2_
  79.5 0.0 collective-permute-done.3.refs_1_
  79.5 6.2 %all-to-all-start.1 = ((bf16[16,32,896]{2,1,0:T(8,128)(2,1)}), bf16[16,32,896]{2,1,0:T(8,128)(2,1)S(1)}, u32[]{:S(2)}, u32[]{:S(2)}) async-start(bf16[16,32,896]{2,1,0:T(8,128)(2,1)} %bitcast.5), calls=%async_computation.1 | async-start | bytes 1835008 | tf_op jit(solution)/shard_map/all_to_all | solution.py:156
  85.7 1.9 %collective-permute-start.5 = (bf16[448,1024]{1,0:T(8,128)(2,1)}, bf16[448,1024]{1,0:T(8,128)(2,1)S(1)}, u32[]{:S(2)}, u32[]{:S(2)}) collective-permute-start(bf16[448,1024]{1,0:T(8,128)(2,1)} %collective-permute-done.4.refs_2_), channel_id=1, source_target_pairs={{0,8},{8,0},{1,9},{9,1},{2,10},{10,2},{3,11},{11,3},{4,12},{12,4},... | collective-permute-start | bytes 2752520 | tf_op jit(solution)/shard_map/ppermute | solution.py:155
  87.6 2.6 %collective-permute-done.5.refs_3_ = bf16[448,1024]{1,0:T(8,128)(2,1)S(1)} collective-permute-done((bf16[448,1024]{1,0:T(8,128)(2,1)}, bf16[448,1024]{1,0:T(8,128)(2,1)S(1)}, u32[]{:S(2)}, u32[]{:S(2)}) %collective-permute-start.5) | collective-permute-done | bytes 917536 | tf_op jit(solution)/shard_map/ppermute | solution.py:155
  90.3 3.9 %all-to-all-done.1 = bf16[16,32,896]{2,1,0:T(8,128)(2,1)S(1)} async-done(((bf16[16,32,896]{2,1,0:T(8,128)(2,1)}), bf16[16,32,896]{2,1,0:T(8,128)(2,1)S(1)}, u32[]{:S(2)}, u32[]{:S(2)}) %all-to-all-start.1) | async-done | bytes 917536 | tf_op jit(solution)/shard_map/all_to_all | solution.py:156
  94.1 2.5 %shard_map.49 = bf16[256,1024]{1,0:T(8,128)(2,1)S(1)} custom-call(s32[1]{0:T(128)} %bitcast.at_zb_ref, bf16[8,2,32,896]{3,2,1,0:T(8,128)(2,1)S(1)} %bitcast.15, bf16[448,1024]{1,0:T(8,128)(2,1)S(1)} %copy-done.4, bf16[448,1024]{1,0:T(8,128)(2,1)} %collective-permute-done.3.refs_1_, bf16[448,1024]{1,0:T(8,128)(2,1)} %collective-permute-done.4.refs_2_, ...), custom_call_target="tpu_custom_call" | custom-call | flops 939524096 | bytes 4587522 | tf_op jit(solution)/shard_map/pallas_call | solution.py:103
  96.6 15.5 %all_to_all.20 = bf16[4,64,1024]{2,1,0:T(8,128)(2,1)S(1)} all-to-all(bf16[4,64,1024]{2,1,0:T(8,128)(2,1)S(1)} %bitcast.16), channel_id=1, replica_groups={{0,448,16,464},{8,456,24,472},{32,480,48,496},{40,488,56,504},{192,256,..., dimensions={0} | all-to-all | bytes 1048576 | tf_op jit(solution)/shard_map/all_to_all | solution.py:171
  112.1 0.1 reduce_sum.24
  112.2 19.1 %all_to_all.21 = bf16[4,16,1024]{2,1,0:T(8,128)(2,1)S(1)} all-to-all(bf16[4,16,1024]{2,1,0:T(8,128)(2,1)S(1)} %bitcast.17), channel_id=1, replica_groups={{0,192,384,64},{8,200,392,72},{16,208,400,80},{24,216,408,88},{32,224,4..., dimensions={0} | all-to-all | bytes 262144 | tf_op jit(solution)/shard_map/all_to_all | solution.py:172
  131.3 0.6 reduce_sum.25
Async XLA Ops:
  0.0 48.1 %collective-permute-start.1 = (bf16[448,1024]{1,0:T(8,128)(2,1)}, bf16[448,1024]{1,0:T(8,128)(2,1)S(1)}, u32[]{:S(2)}, u32[]{:S(2)}) collective-permute-start(bf16[448,1024]{1,0:T(8,128)(2,1)} %bitcast.9), channel_id=1, source_target_pairs={{0,8},{8,0},{1,9},{9,1},{2,10},{10,2},{3,11},{11,3},{4,12},{12,4},... | collective-permute-start | bytes 2752520 | tf_op jit(solution)/shard_map/ppermute | solution.py:123
  1.9 46.2 %collective-permute-start.2 = (bf16[448,1024]{1,0:T(8,128)(2,1)}, bf16[448,1024]{1,0:T(8,128)(2,1)S(1)}, u32[]{:S(2)}, u32[]{:S(2)}) collective-permute-start(bf16[448,1024]{1,0:T(8,128)(2,1)} %bitcast.12), channel_id=1, source_target_pairs={{0,8},{8,0},{1,9},{9,1},{2,10},{10,2},{3,11},{11,3},{4,12},{12,4},... | collective-permute-start | bytes 2752520 | tf_op jit(solution)/shard_map/ppermute | solution.py:123
  43.2 12.6 %collective-permute-start = (bf16[256,1024]{1,0:T(8,128)(2,1)S(1)}, bf16[256,1024]{1,0:T(8,128)(2,1)S(1)}, u32[]{:S(2)}, u32[]{:S(2)}) collective-permute-start(bf16[256,1024]{1,0:T(8,128)(2,1)S(1)} %all_gather.3.x_ref), channel_id=1, source_target_pairs={{0,16},{16,0},{1,17},{17,1},{2,18},{18,2},{3,19},{19,3},{4,20},{20... | collective-permute-start | bytes 1572872 | tf_op jit(solution)/shard_map/ppermute | solution.py:127
  48.1 1.2 copy-start
  49.3 1.2 copy-start.2
  50.5 5.3 %copy-start.1 = (bf16[1024,448]{0,1:T(8,128)(2,1)S(1)}, bf16[1024,448]{0,1:T(8,128)(2,1)}, u32[]{:S(2)}) copy-start(bf16[1024,448]{0,1:T(8,128)(2,1)} %param.5) | copy-start | bytes 2752516
  50.5 5.3 %copy-start.3 = (bf16[1024,448]{0,1:T(8,128)(2,1)S(1)}, bf16[1024,448]{0,1:T(8,128)(2,1)}, u32[]{:S(2)}) copy-start(bf16[1024,448]{0,1:T(8,128)(2,1)} %param.6) | copy-start | bytes 2752516
  57.9 5.9 %copy-start.4 = (bf16[448,1024]{1,0:T(8,128)(2,1)S(1)}, bf16[448,1024]{1,0:T(8,128)(2,1)}, u32[]{:S(2)}) copy-start(bf16[448,1024]{1,0:T(8,128)(2,1)} %refs_0_) | copy-start | bytes 2752516
  57.9 19.9 %all-to-all-start = ((bf16[8,2,32,1792]{3,2,1,0:T(8,128)(2,1)}), bf16[8,2,32,1792]{3,2,1,0:T(8,128)(2,1)S(1)}, u32[]{:S(2)}, u32[]{:S(2)}) async-start(bf16[8,2,32,1792]{3,2,1,0:T(8,128)(2,1)} %bitcast.4), calls=%async_computation | async-start | bytes 3670016 | tf_op jit(solution)/shard_map/all_to_all | solution.py:152
  63.8 15.6 %collective-permute-start.4 = (bf16[448,1024]{1,0:T(8,128)(2,1)S(1)}, bf16[448,1024]{1,0:T(8,128)(2,1)}, u32[]{:S(2)}, u32[]{:S(2)}) collective-permute-start(bf16[448,1024]{1,0:T(8,128)(2,1)S(1)} %copy-done.4), channel_id=1, source_target_pairs={{0,32},{32,0},{1,33},{33,1},{2,34},{34,2},{3,35},{35,3},{4,36},{36... | collective-permute-start | bytes 2752520 | tf_op jit(solution)/shard_map/ppermute | solution.py:150
  65.7 13.7 %collective-permute-start.3 = (bf16[448,1024]{1,0:T(8,128)(2,1)S(1)}, bf16[448,1024]{1,0:T(8,128)(2,1)}, u32[]{:S(2)}, u32[]{:S(2)}) collective-permute-start(bf16[448,1024]{1,0:T(8,128)(2,1)S(1)} %copy-done.4), channel_id=1, source_target_pairs={{0,8},{8,0},{1,9},{9,1},{2,10},{10,2},{3,11},{11,3},{4,12},{12,4},... | collective-permute-start | bytes 2752520 | tf_op jit(solution)/shard_map/ppermute | solution.py:151
  79.5 14.7 %all-to-all-start.1 = ((bf16[16,32,896]{2,1,0:T(8,128)(2,1)}), bf16[16,32,896]{2,1,0:T(8,128)(2,1)S(1)}, u32[]{:S(2)}, u32[]{:S(2)}) async-start(bf16[16,32,896]{2,1,0:T(8,128)(2,1)} %bitcast.5), calls=%async_computation.1 | async-start | bytes 1835008 | tf_op jit(solution)/shard_map/all_to_all | solution.py:156
  85.7 4.6 %collective-permute-start.5 = (bf16[448,1024]{1,0:T(8,128)(2,1)}, bf16[448,1024]{1,0:T(8,128)(2,1)S(1)}, u32[]{:S(2)}, u32[]{:S(2)}) collective-permute-start(bf16[448,1024]{1,0:T(8,128)(2,1)} %collective-permute-done.4.refs_2_), channel_id=1, source_target_pairs={{0,8},{8,0},{1,9},{9,1},{2,10},{10,2},{3,11},{11,3},{4,12},{12,4},... | collective-permute-start | bytes 2752520 | tf_op jit(solution)/shard_map/ppermute | solution.py:155
